TPU v7x, 32 devices: a whole 2x2x4 slice. The times are simulated.
32 devices in a mesh: grp: 8 (over z, core), exp: 4 (over y, x).
Axes of the slice: x: 2, y: 2, z: 4, core: 2. Of those that a mesh axis runs over, the one named last changes fastest.
Arguments:
- hidden: bfloat16 [8, 16, 7168], P('grp', 'exp'), may hold values from -6 to 6
- norm_gain: float32 [7168], replicated, may hold values from 0.1 to 1.9
- route: int32 [8, 16, 1], P('grp', 'exp'), may hold values from 0 to 1; in each aligned block of 4 rows (0 to 3, 4 to 7, ..., all dimensions but the last counted through in order) at most 3 rows name the same one
- route_weight: float32 [8, 16], P('grp', 'exp'), may hold values from 0.2 to 1
- resident: bfloat16 [2, 2048, 7168], P(None, 'exp'), may hold values from -0.0625 to 0.0625
- sectioned: bfloat16 [8, 512, 7168], P('grp', 'exp'), may hold values from -0.1875 to 0.1875
- owner: int32 [8], replicated, may hold values from 0 to 7, each once
Outputs:
- moe_out: bfloat16 [8, 16, 7168], P('grp', 'exp')
Inputs may be any that keep to these rules, and one draw needn't show every extreme that they name: `route`: each row names one of the 2 experts. Among the 4 rows of one device at most 3 name the same expert, and in every draw some device has exactly 3 rows naming one expert. Every group number appears exactly once, so the 4 buckets have distinct owner groups.
All inputs are finite; a program needn't handle non-finite values.
Results may differ from a plain program's by a relative error of at most 0.0071.
Values may be sent and summed in bfloat16 or wider, within the bound.
No kernel may reach another device: no remote copies, remote signals or barrier semaphores. Data moves between devices by JAX's collectives and lax.ppermute only.
A program may use at most 64 MiB of HBM per device.

v0:
```python
import functools

import jax
import jax.numpy as jnp
from jax import lax
from jax.experimental import pallas as pl
from jax.experimental.pallas import tpu as pltpu
from jax.sharding import PartitionSpec as P


E_WIN = 2
BUCKETS = 4
CAP = 3
PAIR = 2


epsilon = 1e-06


def from_root(value, axis, source):
    kept = jnp.where(lax.axis_index(axis) == source, value, 0).astype(value.dtype)
    return lax.psum(kept, axis)


def activate(slot_rows, gate_up):
    gate_part = lax.dot_general(
        slot_rows, gate_up[0], (((1,), (1,)), ((), ())), preferred_element_type=jnp.float32
    )
    up_part = lax.dot_general(
        slot_rows, gate_up[1], (((1,), (1,)), ((), ())), preferred_element_type=jnp.float32
    )
    return (jax.nn.silu(gate_part) * up_part).astype(jnp.bfloat16)


def normalize(rows, norm_gain):
    row_data = rows.astype(jnp.float32)
    scale = lax.rsqrt(jnp.mean(row_data * row_data, axis=1, keepdims=True) + epsilon)
    return (row_data * scale * norm_gain[None, :]).astype(jnp.bfloat16)


def move_weights(hidden, norm_gain, route, route_weight, resident, sectioned, owner):
    normed = normalize(hidden[0], norm_gain)
    row_count, width = normed.shape
    devices = lax.axis_size("exp")
    shards = devices // E_WIN
    expert_ids = route[0, :, 0]
    onehot = (expert_ids[:, None] == jnp.arange(E_WIN, dtype=jnp.int32)[None, :]).astype(jnp.int32)
    position = jnp.cumsum(onehot, axis=0) - onehot
    slot_index = jnp.sum(position * onehot, axis=1)
    placing = onehot[:, :, None] * (
        slot_index[:, None, None] == jnp.arange(CAP, dtype=jnp.int32)[None, None, :]
    ).astype(jnp.int32)
    placing = placing.reshape(row_count, E_WIN * CAP)
    packed = jnp.dot(
        placing.astype(jnp.bfloat16).T, normed, preferred_element_type=jnp.float32
    ).astype(jnp.bfloat16)
    packed = packed.reshape(E_WIN, 1, CAP, width)
    outgoing = jnp.broadcast_to(packed, (E_WIN, shards, CAP, width)).reshape(devices, CAP, width)
    piece_rows = sectioned.shape[1]
    arrived = lax.all_to_all(outgoing, "exp", split_axis=0, concat_axis=0, tiled=True)
    flat_slots = arrived.reshape(-1, width)
    activation = activate(flat_slots, resident)
    running_sum = jnp.zeros((flat_slots.shape[0], width), jnp.float32)
    for bucket in range(BUCKETS):
        weight_piece = from_root(sectioned[0], "grp", owner[bucket])
        act_piece = activation[:, bucket * piece_rows : (bucket + 1) * piece_rows]
        running_sum = running_sum + jnp.dot(
            act_piece, weight_piece, preferred_element_type=jnp.float32
        )
    partials = running_sum.astype(jnp.bfloat16).reshape(arrived.shape)
    returned = lax.all_to_all(partials, "exp", split_axis=0, concat_axis=0, tiled=True)
    summed = jnp.sum(returned.astype(jnp.float32).reshape(E_WIN, shards, CAP, width), axis=1)
    summed = summed.reshape(E_WIN * CAP, width)
    combined = jnp.dot(placing.astype(jnp.float32), summed, precision=lax.Precision.HIGHEST)
    result = (combined * route_weight[0][:, None]).astype(jnp.bfloat16)
    return result.reshape(1, row_count, width)


def swap(value, axis, bits):
    size = lax.axis_size(axis)
    return lax.ppermute(value, axis, [(i, i ^ bits) for i in range(size)])


NT = (((1,), (1,)), ((), ()))
VMEM = pl.BlockSpec(memory_space=pltpu.VMEM)
ANY = pl.BlockSpec(memory_space=pl.ANY)
HBM = pl.BlockSpec(memory_space=pltpu.HBM)
CODE = 128
MIB = 1 << 20


def held(*values):
    return [pltpu.with_memory_space_constraint(value, pltpu.VMEM) for value in values]


def in_hbm(*values):
    return [pltpu.with_memory_space_constraint(value, pltpu.HBM) for value in values]


def limit(mib):
    return pltpu.CompilerParams(vmem_limit_bytes=mib * MIB)


def prepare_body(shards, route_hbm, rows_hbm, gain_hbm, *refs):
    blocks, code_ref = refs[:E_WIN], refs[E_WIN]
    route_ref, rows_ref, gain_ref, sems = refs[E_WIN + 1 :]
    copies = [
        pltpu.make_async_copy(source, target, sems.at[index])
        for index, (source, target) in enumerate(
            ((rows_hbm, rows_ref), (gain_hbm, gain_ref), (route_hbm, route_ref))
        )
    ]
    for copy in copies:
        copy.start()
    for copy in copies:
        copy.wait()
    row_count, width = rows_ref.shape
    rows = rows_ref[...].astype(jnp.float32)
    scale = lax.rsqrt(jnp.sum(rows * rows, axis=1, keepdims=True) * (1.0 / width) + epsilon)
    normed = (rows * scale * gain_ref[...]).astype(jnp.bfloat16)
    named = [route_ref[0, row] for row in range(row_count)]
    at = lax.broadcasted_iota(jnp.int32, code_ref.shape, 1)
    code = jnp.full(code_ref.shape, -1, jnp.int32)
    for row in range(row_count):
        slot = jnp.int32(0)
        for before in range(row):
            slot = slot + jnp.where(named[before] == named[row], 1, 0)
        code = jnp.where(at == row, named[row] * row_count + slot, code)
    code_ref[...] = code.astype(jnp.float32)
    mine = lax.axis_index("exp") // shards
    height = E_WIN * row_count
    row = lax.broadcasted_iota(jnp.int32, (height, CODE), 0)
    wanted = (mine ^ (row // row_count)) * row_count + row % row_count
    placing = jnp.where(wanted == code[0:1], 1.0, 0.0).astype(jnp.bfloat16)[:, :row_count]
    packed = jnp.dot(placing, normed, preferred_element_type=jnp.float32)
    for expert in range(E_WIN):
        blocks[expert][...] = packed[expert * row_count : (expert + 1) * row_count].astype(
            jnp.bfloat16
        )


def flag_body(chips, row_count, owner, after, flags, placing, owner_ref, sems):
    owner_copy = pltpu.make_async_copy(owner, owner_ref, sems.at[0])
    owner_copy.start()
    shape = placing.shape[1:]
    row, column = (lax.broadcasted_iota(jnp.int32, shape, axis) for axis in (0, 1))
    block, used = 2 * CAP * chips, shape[0] // 2
    lower, home, spot = row // used, (row % used) // block, row % block
    slot, part, at = spot // (2 * chips), (spot % (2 * chips)) // chips, spot % chips
    matches = (part == lower) & (home == column // row_count) & (slot == column % row_count)
    for chip in range(chips):
        placing[chip] = jnp.where(matches & (at == chip), 1.0, 0.0).astype(jnp.bfloat16)
    owner_copy.wait()
    group = lax.axis_index("grp")
    row = lax.broadcasted_iota(jnp.int32, flags.shape, 0)
    values = jnp.zeros(flags.shape, jnp.float32)
    for which in range(PAIR):
        for bucket in range(BUCKETS):
            hit = jnp.where(owner_ref[0, bucket] == (group ^ which), 1.0, 0.0)
            values = jnp.where(row == which * BUCKETS + bucket, hit, values)
    flags[...] = values


def activate_body(devices, weights, code_ref, *refs):
    blocks, out, stacked = refs[:devices], refs[devices], refs[devices + 1]
    row_count = blocks[0].shape[0]
    for index in range(devices):
        stacked[index * row_count : (index + 1) * row_count, :] = blocks[index][...].astype(
            jnp.float32
        )
    rows = stacked[...].astype(jnp.bfloat16)
    width = rows.shape[1]
    step = width // 4 if width % 512 == 0 else width
    gate, up = 0.0, 0.0
    for start in range(0, width, step):
        part = rows[:, start : start + step]
        gate = gate + lax.dot_general(
            part, weights[0, :, start : start + step], NT, preferred_element_type=jnp.float32
        )
        up = up + lax.dot_general(
            part, weights[1, :, start : start + step], NT, preferred_element_type=jnp.float32
        )
    act = gate * jax.nn.sigmoid(gate) * up
    spare = lax.broadcasted_iota(jnp.int32, (act.shape[0], CODE), 0) == CAP
    out[:, :CODE] = jnp.where(spare, code_ref[0:1, :], act[:, :CODE]).astype(jnp.bfloat16)
    out[:, CODE:] = act[:, CODE:].astype(jnp.bfloat16)


def down_body(devices, chips, own, other, flags, placing, *refs):
    acts, partials = refs[:chips], refs[chips:]
    block, half = partials[0].shape
    used = devices * block
    rows, units = acts[0].shape
    piece = units // BUCKETS
    placed = [jnp.zeros((2 * used, piece), jnp.float32) for _ in range(PAIR)]
    for chip in range(chips):
        for which in range(PAIR):
            chosen = jnp.zeros((rows, piece), jnp.float32)
            for bucket in range(BUCKETS):
                flag = flags[which * BUCKETS + bucket : which * BUCKETS + bucket + 1, 0:piece]
                piece_of = acts[chip][:, bucket * piece : (bucket + 1) * piece].astype(jnp.float32)
                chosen = jnp.where(flag > 0.5, piece_of, chosen)
            placed[which] = placed[which] + jnp.dot(
                placing[chip], chosen.astype(jnp.bfloat16), preferred_element_type=jnp.float32
            )
    placed = [part.astype(jnp.bfloat16) for part in placed]
    step = half // 7 if half % (7 * 128) == 0 else half
    for start in range(0, half, step):
        out = 0.0
        for rows_at, column in ((0, start), (used, half + start)):
            for part, weights in zip(placed, (own, other)):
                out = out + jnp.dot(
                    part[rows_at : rows_at + used],
                    weights[:, column : column + step],
                    preferred_element_type=jnp.float32,
                )
        for index in range(devices):
            partials[index][:, start : start + step] = out[
                index * block : (index + 1) * block
            ].astype(jnp.bfloat16)


def place_body(chips, shards, row_count, block, *refs):
    acts, placing, codes = refs[:chips], refs[-2], refs[-1]
    mine = lax.axis_index("exp") // shards
    diagonal = lax.broadcasted_iota(jnp.int32, (row_count, CODE), 0) == lax.broadcasted_iota(
        jnp.int32, (row_count, CODE), 1
    )
    for chip in range(chips):
        line = acts[chip][:, :CODE].astype(jnp.float32)[CAP : CAP + 1, :]
        mark = jnp.sum(jnp.where(diagonal, line, 0.0), axis=1, keepdims=True)
        codes[chip * row_count : (chip + 1) * row_count, :] = jnp.broadcast_to(
            mark, (row_count, CODE)
        )
    code = codes[...]
    home = lax.broadcasted_iota(jnp.int32, code.shape, 0) // row_count
    at = lax.broadcasted_iota(jnp.int32, code.shape, 1)
    at_slot, at_part, at_chip = at // (2 * chips), (at % (2 * chips)) // chips, at % chips
    for expert in range(E_WIN):
        wanted = ((mine ^ expert) * row_count + at_slot).astype(jnp.float32)
        chosen = (wanted == code) & (at_chip == home) & (at < block)
        for part in range(2):
            placing[2 * expert + part] = jnp.where(chosen & (at_part == part), 1.0, 0.0).astype(
                jnp.bfloat16
            )


def combine_body(devices, chips, shards, placing, *refs):
    blocks, outs = refs[:devices], refs[devices:]
    block, half = blocks[0].shape
    row_count = outs[0].shape[0]
    for part in range(2):
        total = 0.0
        for index in range(devices):
            total = total + jnp.dot(
                placing[2 * (index // shards) + part][:, :block],
                blocks[index][...],
                preferred_element_type=jnp.float32,
            )
        for chip in range(chips):
            outs[chip][:, part * half : (part + 1) * half] = total[
                chip * row_count : (chip + 1) * row_count
            ].astype(outs[chip].dtype)


def exchange(values, axis):
    groups, devices = lax.axis_size("grp"), lax.axis_size("exp")
    moved = [values[0]]
    for bits in range(1, len(values)):
        group_bits, bits_along = (1, bits) if axis == "exp" else (PAIR * bits + 1, 0)
        pairs = [
            (group * devices + index, (group ^ group_bits) * devices + (index ^ bits_along))
            for group in range(groups)
            for index in range(devices)
        ]
        moved.append(lax.ppermute(values[bits], ("grp", "exp"), pairs))
    return moved


def move_rows(hidden, norm_gain, route, route_weight, resident, sectioned, owner):
    rows, own_piece = hidden[0], sectioned[0]
    row_count, width = rows.shape
    devices = lax.axis_size("exp")
    chips = lax.axis_size("grp") // PAIR
    shards = devices // E_WIN
    half, block = width // 2, 2 * CAP * chips
    units = resident.shape[1]
    row_block = pltpu.VMEM((row_count, width), jnp.bfloat16)
    *packed, code = pl.pallas_call(
        functools.partial(prepare_body, shards),
        out_shape=[row_block] * E_WIN + [pltpu.VMEM((8, CODE), jnp.float32)],
        in_specs=[HBM] * 3,
        out_specs=[VMEM] * (E_WIN + 1),
        scratch_shapes=[
            pltpu.SMEM((1, row_count), jnp.int32),
            pltpu.VMEM((row_count, width), jnp.bfloat16),
            pltpu.VMEM((1, width), jnp.float32),
            pltpu.SemaphoreType.DMA((3,)),
        ],
        compiler_params=limit(4),
        cost_estimate=pl.CostEstimate(flops=10**10, transcendentals=0, bytes_accessed=2 * 10**7),
        name="prepare",
    )(*in_hbm(route.reshape(1, row_count), rows, norm_gain.reshape(1, width)))
    arrived = exchange([packed[bits // shards] for bits in range(devices)], "exp")
    other_piece = swap(own_piece, "grp", 1)
    flags, spots = pl.pallas_call(
        functools.partial(flag_body, chips, row_count),
        out_shape=[
            pltpu.VMEM((8, CODE), jnp.float32),
            pltpu.VMEM((chips, 2 * devices * block, devices * row_count), jnp.bfloat16),
        ],
        in_specs=[HBM, ANY],
        out_specs=[VMEM] * 2,
        scratch_shapes=[pltpu.SMEM((1, owner.shape[0]), jnp.int32), pltpu.SemaphoreType.DMA((1,))],
        compiler_params=limit(2),
        name="flag",
    )(*in_hbm(owner.reshape(1, -1)), *held(code))
    act = pl.pallas_call(
        functools.partial(activate_body, devices),
        out_shape=pltpu.VMEM((devices * row_count, units), jnp.bfloat16),
        in_specs=[VMEM] * (2 + devices),
        out_specs=VMEM,
        scratch_shapes=[pltpu.VMEM((devices * row_count, width), jnp.float32)],
        compiler_params=limit(20),
        name="activate",
    )(resident, *held(code, *arrived))
    acts = exchange([act] * chips, "grp")
    half_block = pltpu.VMEM((block, half), jnp.bfloat16)
    partials = pl.pallas_call(
        functools.partial(down_body, devices, chips),
        out_shape=[half_block] * devices,
        in_specs=[VMEM] * (4 + chips),
        out_specs=[VMEM] * devices,
        compiler_params=limit(12),
        name="down",
    )(*held(own_piece, other_piece, flags, spots, *acts))
    returned = exchange(partials, "exp")
    placing = pl.pallas_call(
        functools.partial(place_body, chips, shards, row_count, block),
        out_shape=pltpu.VMEM((2 * E_WIN, chips * row_count, CODE), jnp.bfloat16),
        in_specs=[VMEM] * chips + [ANY],
        out_specs=VMEM,
        scratch_shapes=[pltpu.VMEM((chips * row_count, CODE), jnp.float32)],
        compiler_params=limit(2),
        name="place",
    )(*held(*acts, partials[0]))
    sums = pl.pallas_call(
        functools.partial(combine_body, devices, chips, shards),
        out_shape=[row_block] * chips,
        in_specs=[VMEM] * (1 + devices),
        out_specs=[VMEM] * chips,
        compiler_params=limit(8),
        name="combine",
    )(*held(placing, *returned))
    combined = 0.0
    for share in exchange(sums, "grp"):
        combined = combined + share.astype(jnp.float32)
    result = (combined * route_weight[0][:, None]).astype(jnp.bfloat16)
    return result.reshape(1, row_count, width)


def per_device(hidden, norm_gain, route, route_weight, resident, sectioned, owner):
    weight_rows = BUCKETS * sectioned.shape[1]
    partial_rows = lax.axis_size("exp") * lax.axis_size("grp") // PAIR * hidden.shape[1]
    plan = move_rows if partial_rows < weight_rows else move_weights
    return plan(hidden, norm_gain, route, route_weight, resident, sectioned, owner)


def solution(mesh):
    in_specs = (
        P("grp", "exp", None),
        P(),
        P("grp", "exp", None),
        P("grp", "exp"),
        P(None, "exp", None),
        P("grp", "exp", None),
        P(),
    )
    out_specs = P("grp", "exp", None)
    return jax.shard_map(
        per_device, mesh=mesh, in_specs=in_specs, out_specs=out_specs, check_vma=False
    )
```

profile of v0, /device:TPU:0, one launch (start us, length us, event | category | flops | bytes accessed | tf_op | source)
XLA Modules:
  0.0 42.8 jit_solution(18321654966729170571)
XLA Ops:
  0.0 0.5 %collective-permute-start.6 = (bf16[128,7168]{1,0:T(8,128)(2,1)}, bf16[128,7168]{1,0:T(8,128)(2,1)S(1)}, u32[]{:S(2)}, u32[]{:S(2)}) collective-permute-start(bf16[128,7168]{1,0:T(8,128)(2,1)} %bitcast.10), channel_id=1, source_target_pairs={{0,4},{4,0},{8,12},{12,8},{16,20},{20,16},{24,28},{28,24},{1,5},{5... | collective-permute-start | bytes 5505032 | tf_op jit(solution)/shard_map/ppermute | solution.py:81
  0.5 0.0 slice-start
  0.5 0.0 slice-start.1
  0.5 0.0 slice-start.2
  0.5 0.0 slice-start.3
  0.5 1.4 %prepare.1 = (bf16[4,7168]{1,0:T(4,128)(2,1)S(1)}, bf16[4,7168]{1,0:T(4,128)(2,1)S(1)}, f32[8,128]{1,0:T(8,128)S(1)}) custom-call(s32[1,4]{1,0:T(1,128)} %bitcast.16, bf16[4,7168]{1,0:T(4,128)(2,1)} %bitcast.14, f32[1,7168]{1,0:T(1,128)} %bitcast.15), custom_call_target="tpu_custom_call" | custom-call | flops 10000000000 | bytes 20000000 | tf_op jit(solution)/shard_map/prepare/pallas_call | solution.py:289
  1.9 2.7 %collective-permute-start = (bf16[4,7168]{1,0:T(4,128)(2,1)S(1)}, bf16[4,7168]{1,0:T(4,128)(2,1)S(1)}, u32[]{:S(2)}, u32[]{:S(2)}) collective-permute-start(bf16[4,7168]{1,0:T(4,128)(2,1)S(1)} %get-tuple-element.19.refs_0_), channel_id=1, source_target_pairs={{0,5},{1,4},{2,7},{3,6},{4,1},{5,0},{6,3},{7,2},{8,13},{9,12},{10,... | collective-permute-start | bytes 172040 | tf_op jit(solution)/shard_map/ppermute | solution.py:276
  4.5 1.1 %collective-permute-start.2 = (bf16[4,7168]{1,0:T(4,128)(2,1)S(1)}, bf16[4,7168]{1,0:T(4,128)(2,1)S(1)}, u32[]{:S(2)}, u32[]{:S(2)}) collective-permute-start(bf16[4,7168]{1,0:T(4,128)(2,1)S(1)} %get-tuple-element.20), channel_id=1, source_target_pairs={{0,7},{1,6},{2,5},{3,4},{4,3},{5,2},{6,1},{7,0},{8,15},{9,14},{10,... | collective-permute-start | bytes 172040 | tf_op jit(solution)/shard_map/ppermute | solution.py:276
  5.6 0.1 collective-permute-start.1
  5.7 1.1 %collective-permute-done.refs_1_ = bf16[4,7168]{1,0:T(4,128)(2,1)S(1)} collective-permute-done((bf16[4,7168]{1,0:T(4,128)(2,1)S(1)}, bf16[4,7168]{1,0:T(4,128)(2,1)S(1)}, u32[]{:S(2)}, u32[]{:S(2)}) %collective-permute-start) | collective-permute-done | bytes 57376 | tf_op jit(solution)/shard_map/ppermute | solution.py:276
  6.8 2.7 %collective-permute-done.2.refs_3_ = bf16[4,7168]{1,0:T(4,128)(2,1)S(1)} collective-permute-done((bf16[4,7168]{1,0:T(4,128)(2,1)S(1)}, bf16[4,7168]{1,0:T(4,128)(2,1)S(1)}, u32[]{:S(2)}, u32[]{:S(2)}) %collective-permute-start.2) | collective-permute-done | bytes 57376 | tf_op jit(solution)/shard_map/ppermute | solution.py:276
  9.5 1.3 %collective-permute-done.1.refs_2_ = bf16[4,7168]{1,0:T(4,128)(2,1)S(1)} collective-permute-done((bf16[4,7168]{1,0:T(4,128)(2,1)S(1)}, bf16[4,7168]{1,0:T(4,128)(2,1)S(1)}, u32[]{:S(2)}, u32[]{:S(2)}) %collective-permute-start.1) | collective-permute-done | bytes 57376 | tf_op jit(solution)/shard_map/ppermute | solution.py:276
  10.8 0.0 slice-done
  10.8 0.0 slice-done.1
  10.8 0.0 slice-done.2
  10.8 0.0 slice-done.3
  10.8 0.0 copy-start
  10.8 3.9 %activate.1.refs_0_ = bf16[16,512]{1,0:T(8,128)(2,1)S(1)} custom-call(bf16[2,512,7168]{2,1,0:T(8,128)(2,1)S(1)} %bitcast.9, f32[8,128]{1,0:T(8,128)S(1)} %get-tuple-element.18.code_ref.after, bf16[4,7168]{1,0:T(4,128)(2,1)S(1)} %get-tuple-element.19.refs_0_, bf16[4,7168]{1,0:T(4,128)(2,1)S(1)} %collective-permute-done.refs_1_, ...), custom_call_target="tpu_custom_call" | custom-call | tf_op jit(solution)/shard_map/activate/pallas_call | solution.py:318
  14.7 3.3 %collective-permute-start.5 = (bf16[16,512]{1,0:T(8,128)(2,1)S(1)}, bf16[16,512]{1,0:T(8,128)(2,1)S(1)}, u32[]{:S(2)}, u32[]{:S(2)}) collective-permute-start(bf16[16,512]{1,0:T(8,128)(2,1)S(1)} %activate.1.refs_0_), channel_id=1, source_target_pairs={{0,28},{1,29},{2,30},{3,31},{4,24},{5,25},{6,26},{7,27},{8,20},{9,... | collective-permute-start | bytes 49160 | tf_op jit(solution)/shard_map/ppermute | solution.py:276
  18.1 0.0 collective-permute-start.4
  18.1 0.6 %collective-permute-start.3 = (bf16[16,512]{1,0:T(8,128)(2,1)S(1)}, bf16[16,512]{1,0:T(8,128)(2,1)S(1)}, u32[]{:S(2)}, u32[]{:S(2)}) collective-permute-start(bf16[16,512]{1,0:T(8,128)(2,1)S(1)} %activate.1.refs_0_), channel_id=1, source_target_pairs={{0,12},{1,13},{2,14},{3,15},{4,8},{5,9},{6,10},{7,11},{8,4},{9,5},... | collective-permute-start | bytes 49160 | tf_op jit(solution)/shard_map/ppermute | solution.py:276
  18.7 0.7 %flag.1 = (f32[8,128]{1,0:T(8,128)S(1)}, bf16[4,192,16]{2,1,0:T(8,128)(2,1)S(1)}) custom-call(s32[1,8]{1,0:T(1,128)} %bitcast.13, f32[8,128]{1,0:T(8,128)S(1)} %get-tuple-element.18.code_ref.after), custom_call_target="tpu_custom_call" | custom-call | tf_op jit(solution)/shard_map/flag/pallas_call | solution.py:306
  19.4 0.3 collective-permute-done.5.refs_3_
  19.7 2.4 %collective-permute-done.4.refs_2_ = bf16[16,512]{1,0:T(8,128)(2,1)S(1)} collective-permute-done((bf16[16,512]{1,0:T(8,128)(2,1)S(1)}, bf16[16,512]{1,0:T(8,128)(2,1)S(1)}, u32[]{:S(2)}, u32[]{:S(2)}) %collective-permute-start.4) | collective-permute-done | bytes 16416 | tf_op jit(solution)/shard_map/ppermute | solution.py:276
  22.1 0.0 collective-permute-done.3.refs_1_
  22.1 0.0 collective-permute-done.6.other
  22.2 0.0 copy-done
  22.2 0.0 copy-start.1
  22.2 1.1 %down.1 = (bf16[24,3584]{1,0:T(8,128)(2,1)S(1)}, bf16[24,3584]{1,0:T(8,128)(2,1)S(1)}, bf16[24,3584]{1,0:T(8,128)(2,1)S(1)}, bf16[24,3584]{1,0:T(8,128)(2,1)S(1)}) custom-call(bf16[128,7168]{1,0:T(8,128)(2,1)S(1)} %bitcast.11, bf16[128,7168]{1,0:T(8,128)(2,1)S(1)} %collective-permute-done.6.other, f32[8,128]{1,0:T(8,128)S(1)} %get-tuple-element.21.flags, ...), custom_call_target="tpu_custom_call" | custom-call | tf_op jit(solution)/shard_map/down/pallas_call | solution.py:329
  23.2 1.1 %collective-permute-start.7 = (bf16[24,3584]{1,0:T(8,128)(2,1)S(1)}, bf16[24,3584]{1,0:T(8,128)(2,1)S(1)}, u32[]{:S(2)}, u32[]{:S(2)}) collective-permute-start(bf16[24,3584]{1,0:T(8,128)(2,1)S(1)} %get-tuple-element.24), channel_id=1, source_target_pairs={{0,5},{1,4},{2,7},{3,6},{4,1},{5,0},{6,3},{7,2},{8,13},{9,12},{10,... | collective-permute-start | bytes 516104 | tf_op jit(solution)/shard_map/ppermute | solution.py:276
  24.3 0.8 %collective-permute-start.8 = (bf16[24,3584]{1,0:T(8,128)(2,1)S(1)}, bf16[24,3584]{1,0:T(8,128)(2,1)S(1)}, u32[]{:S(2)}, u32[]{:S(2)}) collective-permute-start(bf16[24,3584]{1,0:T(8,128)(2,1)S(1)} %get-tuple-element.25), channel_id=1, source_target_pairs={{0,6},{1,7},{2,4},{3,5},{4,2},{5,3},{6,0},{7,1},{8,14},{9,15},{10,... | collective-permute-start | bytes 516104 | tf_op jit(solution)/shard_map/ppermute | solution.py:276
  25.1 1.4 %collective-permute-start.9 = (bf16[24,3584]{1,0:T(8,128)(2,1)S(1)}, bf16[24,3584]{1,0:T(8,128)(2,1)S(1)}, u32[]{:S(2)}, u32[]{:S(2)}) collective-permute-start(bf16[24,3584]{1,0:T(8,128)(2,1)S(1)} %get-tuple-element.26), channel_id=1, source_target_pairs={{0,7},{1,6},{2,5},{3,4},{4,3},{5,2},{6,1},{7,0},{8,15},{9,14},{10,... | collective-permute-start | bytes 516104 | tf_op jit(solution)/shard_map/ppermute | solution.py:276
  26.5 0.1 place.1.placing
  26.6 2.8 %collective-permute-done.7.refs_1_ = bf16[24,3584]{1,0:T(8,128)(2,1)S(1)} collective-permute-done((bf16[24,3584]{1,0:T(8,128)(2,1)S(1)}, bf16[24,3584]{1,0:T(8,128)(2,1)S(1)}, u32[]{:S(2)}, u32[]{:S(2)}) %collective-permute-start.7) | collective-permute-done | bytes 172064 | tf_op jit(solution)/shard_map/ppermute | solution.py:276
  29.4 5.0 %collective-permute-done.8.refs_2_ = bf16[24,3584]{1,0:T(8,128)(2,1)S(1)} collective-permute-done((bf16[24,3584]{1,0:T(8,128)(2,1)S(1)}, bf16[24,3584]{1,0:T(8,128)(2,1)S(1)}, u32[]{:S(2)}, u32[]{:S(2)}) %collective-permute-start.8) | collective-permute-done | bytes 172064 | tf_op jit(solution)/shard_map/ppermute | solution.py:276
  34.4 0.0 collective-permute-done.9.refs_3_
  34.4 0.4 combine.1
  34.8 0.1 collective-permute-start.10
  34.9 1.6 %collective-permute-start.11 = (bf16[4,7168]{1,0:T(4,128)(2,1)S(1)}, bf16[4,7168]{1,0:T(4,128)(2,1)S(1)}, u32[]{:S(2)}, u32[]{:S(2)}) collective-permute-start(bf16[4,7168]{1,0:T(4,128)(2,1)S(1)} %get-tuple-element.29), channel_id=1, source_target_pairs={{0,20},{1,21},{2,22},{3,23},{4,16},{5,17},{6,18},{7,19},{8,28},{9,... | collective-permute-start | bytes 172040 | tf_op jit(solution)/shard_map/ppermute | solution.py:276
  36.4 2.3 %collective-permute-start.12 = (bf16[4,7168]{1,0:T(4,128)(2,1)S(1)}, bf16[4,7168]{1,0:T(4,128)(2,1)S(1)}, u32[]{:S(2)}, u32[]{:S(2)}) collective-permute-start(bf16[4,7168]{1,0:T(4,128)(2,1)S(1)} %get-tuple-element.30), channel_id=1, source_target_pairs={{0,28},{1,29},{2,30},{3,31},{4,24},{5,25},{6,26},{7,27},{8,20},{9,... | collective-permute-start | bytes 172040 | tf_op jit(solution)/shard_map/ppermute | solution.py:276
  38.7 0.1 collective-permute-done.10
  38.8 1.1 %collective-permute-done.11 = bf16[4,7168]{1,0:T(4,128)(2,1)S(1)} collective-permute-done((bf16[4,7168]{1,0:T(4,128)(2,1)S(1)}, bf16[4,7168]{1,0:T(4,128)(2,1)S(1)}, u32[]{:S(2)}, u32[]{:S(2)}) %collective-permute-start.11) | collective-permute-done | bytes 57376 | tf_op jit(solution)/shard_map/ppermute | solution.py:276
  39.8 2.2 %collective-permute-done.12 = bf16[4,7168]{1,0:T(4,128)(2,1)S(1)} collective-permute-done((bf16[4,7168]{1,0:T(4,128)(2,1)S(1)}, bf16[4,7168]{1,0:T(4,128)(2,1)S(1)}, u32[]{:S(2)}, u32[]{:S(2)}) %collective-permute-start.12) | collective-permute-done | bytes 57376 | tf_op jit(solution)/shard_map/ppermute | solution.py:276
  42.1 0.0 copy-done.1
  42.1 0.7 %fusion = bf16[1,4,7168]{2,1,0:T(4,128)(2,1)} fusion(bf16[4,7168]{1,0:T(4,128)(2,1)S(1)} %collective-permute-done.12, bf16[4,7168]{1,0:T(4,128)(2,1)S(1)} %collective-permute-done.11, bf16[4,7168]{1,0:T(4,128)(2,1)S(1)} %collective-permute-done.10, bf16[4,7168]{1,0:T(4,128)(2,1)S(1)} %get-tuple-element.27, f32[4]{0:T(128)S(1)} %bitcast.12), kind=kLoop, calls=%fused_computation.1 | loop fusion | flops 258048 | bytes 286736 | tf_op jit(solution)/shard_map/reshape | solution.py:359
  (1 shorter events, 0.0 us)
Async XLA Ops:
  0.0 22.1 %collective-permute-start.6 = (bf16[128,7168]{1,0:T(8,128)(2,1)}, bf16[128,7168]{1,0:T(8,128)(2,1)S(1)}, u32[]{:S(2)}, u32[]{:S(2)}) collective-permute-start(bf16[128,7168]{1,0:T(8,128)(2,1)} %bitcast.10), channel_id=1, source_target_pairs={{0,4},{4,0},{8,12},{12,8},{16,20},{20,16},{24,28},{28,24},{1,5},{5... | collective-permute-start | bytes 5505032 | tf_op jit(solution)/shard_map/ppermute | solution.py:81
  0.5 10.3 %slice-start = ((s8[14680064]{0:T(1024)(128)(4,1)}), s8[4194304]{0:T(1024)(128)(4,1)S(1)}, s32[]{:S(2)}) async-start(s8[14680064]{0:T(1024)(128)(4,1)} %bitcast.8), calls=%async_computation | async-start | bytes 8388608
  0.5 10.3 %slice-start.1 = ((s8[14680064]{0:T(1024)(128)(4,1)}), s8[4194304]{0:T(1024)(128)(4,1)S(1)}, s32[]{:S(2)}) async-start(s8[14680064]{0:T(1024)(128)(4,1)} %bitcast.8), calls=%async_computation.1 | async-start | bytes 8388608
  0.5 10.3 %slice-start.2 = ((s8[14680064]{0:T(1024)(128)(4,1)}), s8[4194304]{0:T(1024)(128)(4,1)S(1)}, s32[]{:S(2)}) async-start(s8[14680064]{0:T(1024)(128)(4,1)} %bitcast.8), calls=%async_computation.2 | async-start | bytes 8388608
  0.5 10.3 %slice-start.3 = ((s8[14680064]{0:T(1024)(128)(4,1)}), s8[2097152]{0:T(1024)(128)(4,1)S(1)}, s32[]{:S(2)}) async-start(s8[14680064]{0:T(1024)(128)(4,1)} %bitcast.8), calls=%async_computation.3 | async-start | bytes 4194304
  1.9 4.9 %collective-permute-start = (bf16[4,7168]{1,0:T(4,128)(2,1)S(1)}, bf16[4,7168]{1,0:T(4,128)(2,1)S(1)}, u32[]{:S(2)}, u32[]{:S(2)}) collective-permute-start(bf16[4,7168]{1,0:T(4,128)(2,1)S(1)} %get-tuple-element.19.refs_0_), channel_id=1, source_target_pairs={{0,5},{1,4},{2,7},{3,6},{4,1},{5,0},{6,3},{7,2},{8,13},{9,12},{10,... | collective-permute-start | bytes 172040 | tf_op jit(solution)/shard_map/ppermute | solution.py:276
  4.5 5.0 %collective-permute-start.2 = (bf16[4,7168]{1,0:T(4,128)(2,1)S(1)}, bf16[4,7168]{1,0:T(4,128)(2,1)S(1)}, u32[]{:S(2)}, u32[]{:S(2)}) collective-permute-start(bf16[4,7168]{1,0:T(4,128)(2,1)S(1)} %get-tuple-element.20), channel_id=1, source_target_pairs={{0,7},{1,6},{2,5},{3,4},{4,3},{5,2},{6,1},{7,0},{8,15},{9,14},{10,... | collective-permute-start | bytes 172040 | tf_op jit(solution)/shard_map/ppermute | solution.py:276
  5.6 5.2 %collective-permute-start.1 = (bf16[4,7168]{1,0:T(4,128)(2,1)S(1)}, bf16[4,7168]{1,0:T(4,128)(2,1)S(1)}, u32[]{:S(2)}, u32[]{:S(2)}) collective-permute-start(bf16[4,7168]{1,0:T(4,128)(2,1)S(1)} %get-tuple-element.20), channel_id=1, source_target_pairs={{0,6},{1,7},{2,4},{3,5},{4,2},{5,3},{6,0},{7,1},{8,14},{9,15},{10,... | collective-permute-start | bytes 172040 | tf_op jit(solution)/shard_map/ppermute | solution.py:276
  10.8 11.3 %copy-start = (bf16[1,128,7168]{2,1,0:T(8,128)(2,1)S(1)}, bf16[1,128,7168]{2,1,0:T(8,128)(2,1)}, u32[]{:S(2)}) copy-start(bf16[1,128,7168]{2,1,0:T(8,128)(2,1)} %param.12) | copy-start | bytes 5505028
  14.7 5.0 %collective-permute-start.5 = (bf16[16,512]{1,0:T(8,128)(2,1)S(1)}, bf16[16,512]{1,0:T(8,128)(2,1)S(1)}, u32[]{:S(2)}, u32[]{:S(2)}) collective-permute-start(bf16[16,512]{1,0:T(8,128)(2,1)S(1)} %activate.1.refs_0_), channel_id=1, source_target_pairs={{0,28},{1,29},{2,30},{3,31},{4,24},{5,25},{6,26},{7,27},{8,20},{9,... | collective-permute-start | bytes 49160 | tf_op jit(solution)/shard_map/ppermute | solution.py:276
  18.1 4.1 %collective-permute-start.4 = (bf16[16,512]{1,0:T(8,128)(2,1)S(1)}, bf16[16,512]{1,0:T(8,128)(2,1)S(1)}, u32[]{:S(2)}, u32[]{:S(2)}) collective-permute-start(bf16[16,512]{1,0:T(8,128)(2,1)S(1)} %activate.1.refs_0_), channel_id=1, source_target_pairs={{0,20},{1,21},{2,22},{3,23},{4,16},{5,17},{6,18},{7,19},{8,28},{9,... | collective-permute-start | bytes 49160 | tf_op jit(solution)/shard_map/ppermute | solution.py:276
  18.1 4.1 %collective-permute-start.3 = (bf16[16,512]{1,0:T(8,128)(2,1)S(1)}, bf16[16,512]{1,0:T(8,128)(2,1)S(1)}, u32[]{:S(2)}, u32[]{:S(2)}) collective-permute-start(bf16[16,512]{1,0:T(8,128)(2,1)S(1)} %activate.1.refs_0_), channel_id=1, source_target_pairs={{0,12},{1,13},{2,14},{3,15},{4,8},{5,9},{6,10},{7,11},{8,4},{9,5},... | collective-permute-start | bytes 49160 | tf_op jit(solution)/shard_map/ppermute | solution.py:276
  22.2 19.9 %copy-start.1 = (f32[1,4]{1,0:T(1,128)S(1)}, f32[1,4]{1,0:T(1,128)}, u32[]{:S(2)}) copy-start(f32[1,4]{1,0:T(1,128)} %param.10) | copy-start | bytes 52
  23.2 6.2 %collective-permute-start.7 = (bf16[24,3584]{1,0:T(8,128)(2,1)S(1)}, bf16[24,3584]{1,0:T(8,128)(2,1)S(1)}, u32[]{:S(2)}, u32[]{:S(2)}) collective-permute-start(bf16[24,3584]{1,0:T(8,128)(2,1)S(1)} %get-tuple-element.24), channel_id=1, source_target_pairs={{0,5},{1,4},{2,7},{3,6},{4,1},{5,0},{6,3},{7,2},{8,13},{9,12},{10,... | collective-permute-start | bytes 516104 | tf_op jit(solution)/shard_map/ppermute | solution.py:276
  24.3 10.1 %collective-permute-start.8 = (bf16[24,3584]{1,0:T(8,128)(2,1)S(1)}, bf16[24,3584]{1,0:T(8,128)(2,1)S(1)}, u32[]{:S(2)}, u32[]{:S(2)}) collective-permute-start(bf16[24,3584]{1,0:T(8,128)(2,1)S(1)} %get-tuple-element.25), channel_id=1, source_target_pairs={{0,6},{1,7},{2,4},{3,5},{4,2},{5,3},{6,0},{7,1},{8,14},{9,15},{10,... | collective-permute-start | bytes 516104 | tf_op jit(solution)/shard_map/ppermute | solution.py:276
  25.1 9.3 %collective-permute-start.9 = (bf16[24,3584]{1,0:T(8,128)(2,1)S(1)}, bf16[24,3584]{1,0:T(8,128)(2,1)S(1)}, u32[]{:S(2)}, u32[]{:S(2)}) collective-permute-start(bf16[24,3584]{1,0:T(8,128)(2,1)S(1)} %get-tuple-element.26), channel_id=1, source_target_pairs={{0,7},{1,6},{2,5},{3,4},{4,3},{5,2},{6,1},{7,0},{8,15},{9,14},{10,... | collective-permute-start | bytes 516104 | tf_op jit(solution)/shard_map/ppermute | solution.py:276
  34.8 4.0 %collective-permute-start.10 = (bf16[4,7168]{1,0:T(4,128)(2,1)S(1)}, bf16[4,7168]{1,0:T(4,128)(2,1)S(1)}, u32[]{:S(2)}, u32[]{:S(2)}) collective-permute-start(bf16[4,7168]{1,0:T(4,128)(2,1)S(1)} %get-tuple-element.28), channel_id=1, source_target_pairs={{0,12},{1,13},{2,14},{3,15},{4,8},{5,9},{6,10},{7,11},{8,4},{9,5},... | collective-permute-start | bytes 172040 | tf_op jit(solution)/shard_map/ppermute | solution.py:276
  34.9 5.0 %collective-permute-start.11 = (bf16[4,7168]{1,0:T(4,128)(2,1)S(1)}, bf16[4,7168]{1,0:T(4,128)(2,1)S(1)}, u32[]{:S(2)}, u32[]{:S(2)}) collective-permute-start(bf16[4,7168]{1,0:T(4,128)(2,1)S(1)} %get-tuple-element.29), channel_id=1, source_target_pairs={{0,20},{1,21},{2,22},{3,23},{4,16},{5,17},{6,18},{7,19},{8,28},{9,... | collective-permute-start | bytes 172040 | tf_op jit(solution)/shard_map/ppermute | solution.py:276
  36.4 5.7 %collective-permute-start.12 = (bf16[4,7168]{1,0:T(4,128)(2,1)S(1)}, bf16[4,7168]{1,0:T(4,128)(2,1)S(1)}, u32[]{:S(2)}, u32[]{:S(2)}) collective-permute-start(bf16[4,7168]{1,0:T(4,128)(2,1)S(1)} %get-tuple-element.30), channel_id=1, source_target_pairs={{0,28},{1,29},{2,30},{3,31},{4,24},{5,25},{6,26},{7,27},{8,20},{9,... | collective-permute-start | bytes 172040 | tf_op jit(solution)/shard_map/ppermute | solution.py:276
where the time goes:
time: 42.9 us; the launch traced here: 42.8 us
  waiting for transfers between devices  19 us (44%)
  starting transfers between devices  15.4 us (36%)
  Pallas kernels  7.5 us (17%)
  other arithmetic  0.71 us (2%)
    ppermute x12, waiting for transfers between devices, exchange(): moved.append(lax.ppermute(values[bits], ('grp', 'exp'), pairs))  19 us
    ppermute x12, starting transfers between devices, exchange(): moved.append(lax.ppermute(values[bits], ('grp', 'exp'), pairs))  14.9 us
    pallas_call x1, Pallas kernels, move_rows(): pl.pallas_call(functools.partial(activate_body, devices), out_shape=pltpu...  3.91 us
    pallas_call x1, Pallas kernels, move_rows(): pl.pallas_call(functools.partial(prepare_body, shards), out_shape=[row_bl...  1.35 us
    pallas_call x1, Pallas kernels, move_rows(): pl.pallas_call(functools.partial(down_body, devices, chips), out_shape=[h...  1.07 us
  transfers between devices with their start and end apart: 13, of which 10 were waited for; matrix products, arithmetic and copies ran while one was open for 0% of the time, Pallas kernels for 14%

commit v1 on v0

--- a/solution.py
+++ b/solution.py
@@ -101,9 +101,18 @@
     return pltpu.CompilerParams(vmem_limit_bytes=mib * MIB)
 
 
-def prepare_body(shards, route_hbm, rows_hbm, gain_hbm, *refs):
-    blocks, code_ref = refs[:E_WIN], refs[E_WIN]
-    route_ref, rows_ref, gain_ref, sems = refs[E_WIN + 1 :]
+def turned(slot, devices):
+    bits = devices.bit_length() - 1
+    return sum(((slot >> bit) & 1) << (bits - 1 - bit) for bit in range(bits))
+
+
+def expert_shift(slot, devices, shards, odd):
+    return jnp.where(odd, slot // shards, turned(slot, devices) // shards)
+
+
+def prepare_body(devices, shards, route_hbm, rows_hbm, gain_hbm, *refs):
+    blocks, code_ref = refs[:devices], refs[devices]
+    route_ref, rows_ref, gain_ref, sems = refs[devices + 1 :]
     copies = [
         pltpu.make_async_copy(source, target, sems.at[index])
         for index, (source, target) in enumerate(
@@ -128,15 +137,17 @@
         code = jnp.where(at == row, named[row] * row_count + slot, code)
     code_ref[...] = code.astype(jnp.float32)
     mine = lax.axis_index("exp") // shards
-    height = E_WIN * row_count
-    row = lax.broadcasted_iota(jnp.int32, (height, CODE), 0)
-    wanted = (mine ^ (row // row_count)) * row_count + row % row_count
+    odd = lax.axis_index("grp") % PAIR == 1
+    row = lax.broadcasted_iota(jnp.int32, (devices * row_count, CODE), 0)
+    expert = jnp.zeros(row.shape, jnp.int32)
+    for slot in range(devices):
+        named_here = mine ^ expert_shift(slot, devices, shards, odd)
+        expert = jnp.where(row // row_count == slot, named_here, expert)
+    wanted = expert * row_count + row % row_count
     placing = jnp.where(wanted == code[0:1], 1.0, 0.0).astype(jnp.bfloat16)[:, :row_count]
     packed = jnp.dot(placing, normed, preferred_element_type=jnp.float32)
-    for expert in range(E_WIN):
-        blocks[expert][...] = packed[expert * row_count : (expert + 1) * row_count].astype(
-            jnp.bfloat16
-        )
+    for slot in range(devices):
+        blocks[slot][...] = packed[slot * row_count : (slot + 1) * row_count].astype(jnp.bfloat16)
 
 
 def flag_body(chips, row_count, owner, after, flags, placing, owner_ref, sems):
@@ -220,7 +231,7 @@
             ].astype(jnp.bfloat16)
 
 
-def place_body(chips, shards, row_count, block, *refs):
+def place_body(devices, chips, shards, row_count, block, *refs):
     acts, placing, codes = refs[:chips], refs[-2], refs[-1]
     mine = lax.axis_index("exp") // shards
     diagonal = lax.broadcasted_iota(jnp.int32, (row_count, CODE), 0) == lax.broadcasted_iota(
@@ -236,16 +247,18 @@
     home = lax.broadcasted_iota(jnp.int32, code.shape, 0) // row_count
     at = lax.broadcasted_iota(jnp.int32, code.shape, 1)
     at_slot, at_part, at_chip = at // (2 * chips), (at % (2 * chips)) // chips, at % chips
-    for expert in range(E_WIN):
-        wanted = ((mine ^ expert) * row_count + at_slot).astype(jnp.float32)
+    odd = lax.axis_index("grp") % PAIR == 1
+    for slot in range(devices):
+        expert = mine ^ expert_shift(slot, devices, shards, odd)
+        wanted = (expert * row_count + at_slot).astype(jnp.float32)
         chosen = (wanted == code) & (at_chip == home) & (at < block)
         for part in range(2):
-            placing[2 * expert + part] = jnp.where(chosen & (at_part == part), 1.0, 0.0).astype(
+            placing[2 * slot + part] = jnp.where(chosen & (at_part == part), 1.0, 0.0).astype(
                 jnp.bfloat16
             )
 
 
-def combine_body(devices, chips, shards, placing, *refs):
+def combine_body(devices, chips, placing, *refs):
     blocks, outs = refs[:devices], refs[devices:]
     block, half = blocks[0].shape
     row_count = outs[0].shape[0]
@@ -253,7 +266,7 @@
         total = 0.0
         for index in range(devices):
             total = total + jnp.dot(
-                placing[2 * (index // shards) + part][:, :block],
+                placing[2 * index + part][:, :block],
                 blocks[index][...],
                 preferred_element_type=jnp.float32,
             )
@@ -266,14 +279,16 @@
 def exchange(values, axis):
     groups, devices = lax.axis_size("grp"), lax.axis_size("exp")
     moved = [values[0]]
-    for bits in range(1, len(values)):
-        group_bits, bits_along = (1, bits) if axis == "exp" else (PAIR * bits + 1, 0)
-        pairs = [
-            (group * devices + index, (group ^ group_bits) * devices + (index ^ bits_along))
-            for group in range(groups)
-            for index in range(devices)
-        ]
-        moved.append(lax.ppermute(values[bits], ("grp", "exp"), pairs))
+    for turn in range(1, len(values)):
+        pairs = []
+        for group in range(groups):
+            for index in range(devices):
+                if axis == "grp":
+                    there, partner = group ^ (PAIR * turn), index
+                else:
+                    there, partner = group, index ^ (turn if group % PAIR else turned(turn, devices))
+                pairs.append((group * devices + index, there * devices + partner))
+        moved.append(lax.ppermute(values[turn], ("grp", "exp"), pairs))
     return moved
 
 
@@ -287,10 +302,10 @@
     units = resident.shape[1]
     row_block = pltpu.VMEM((row_count, width), jnp.bfloat16)
     *packed, code = pl.pallas_call(
-        functools.partial(prepare_body, shards),
-        out_shape=[row_block] * E_WIN + [pltpu.VMEM((8, CODE), jnp.float32)],
+        functools.partial(prepare_body, devices, shards),
+        out_shape=[row_block] * devices + [pltpu.VMEM((8, CODE), jnp.float32)],
         in_specs=[HBM] * 3,
-        out_specs=[VMEM] * (E_WIN + 1),
+        out_specs=[VMEM] * (devices + 1),
         scratch_shapes=[
             pltpu.SMEM((1, row_count), jnp.int32),
             pltpu.VMEM((row_count, width), jnp.bfloat16),
@@ -301,7 +316,7 @@
         cost_estimate=pl.CostEstimate(flops=10**10, transcendentals=0, bytes_accessed=2 * 10**7),
         name="prepare",
     )(*in_hbm(route.reshape(1, row_count), rows, norm_gain.reshape(1, width)))
-    arrived = exchange([packed[bits // shards] for bits in range(devices)], "exp")
+    arrived = exchange(packed, "exp")
     other_piece = swap(own_piece, "grp", 1)
     flags, spots = pl.pallas_call(
         functools.partial(flag_body, chips, row_count),
@@ -336,8 +351,8 @@
     )(*held(own_piece, other_piece, flags, spots, *acts))
     returned = exchange(partials, "exp")
     placing = pl.pallas_call(
-        functools.partial(place_body, chips, shards, row_count, block),
-        out_shape=pltpu.VMEM((2 * E_WIN, chips * row_count, CODE), jnp.bfloat16),
+        functools.partial(place_body, devices, chips, shards, row_count, block),
+        out_shape=pltpu.VMEM((2 * devices, chips * row_count, CODE), jnp.bfloat16),
         in_specs=[VMEM] * chips + [ANY],
         out_specs=VMEM,
         scratch_shapes=[pltpu.VMEM((chips * row_count, CODE), jnp.float32)],
@@ -345,7 +360,7 @@
         name="place",
     )(*held(*acts, partials[0]))
     sums = pl.pallas_call(
-        functools.partial(combine_body, devices, chips, shards),
+        functools.partial(combine_body, devices, chips),
         out_shape=[row_block] * chips,
         in_specs=[VMEM] * (1 + devices),
         out_specs=[VMEM] * chips,

time: 42.9 us -> 42.6 us (level)
  waiting for transfers between devices: 19 us -> 17.1 us
  starting transfers between devices: 15.4 us -> 17 us
    ppermute x12, waiting for transfers between devices: 19 us -> 17.1 us  [exchange(): moved.append(lax.ppermute(values[turn], ('grp', 'exp'), pairs))]
    ppermute x12, starting transfers between devices: 14.9 us -> 16.5 us  [exchange(): moved.append(lax.ppermute(values[turn], ('grp', 'exp'), pairs))]
  transfers between devices with their start and end apart: 13 -> 13, of which waited for: 10 -> 9; matrix products, arithmetic and copies ran while one was open for 0% -> 0% of each run, Pallas kernels for 14% -> 14%
where the time goes in v1:
time: 42.6 us; the launch traced here: 42.4 us
  waiting for transfers between devices  17.1 us (40%)
  starting transfers between devices  17 us (40%)
  Pallas kernels  7.5 us (18%)
  other arithmetic  0.71 us (2%)
    ppermute x12, waiting for transfers between devices, exchange(): moved.append(lax.ppermute(values[turn], ('grp', 'exp'), pairs))  17.1 us
    ppermute x12, starting transfers between devices, exchange(): moved.append(lax.ppermute(values[turn], ('grp', 'exp'), pairs))  16.5 us
    pallas_call x1, Pallas kernels, move_rows(): pl.pallas_call(functools.partial(activate_body, devices), out_shape=pltpu...  3.91 us
    pallas_call x1, Pallas kernels, move_rows(): pl.pallas_call(functools.partial(prepare_body, devices, shards), out_shap...  1.35 us
    pallas_call x1, Pallas kernels, move_rows(): pl.pallas_call(functools.partial(down_body, devices, chips), out_shape=[h...  1.07 us
  transfers between devices with their start and end apart: 13, of which 9 were waited for; matrix products, arithmetic and copies ran while one was open for 0% of the time, Pallas kernels for 14%

profile of v1, /device:TPU:0, one launch (start us, length us, event | category | flops | bytes accessed | tf_op | source)
XLA Modules:
  0.0 42.4 jit_solution(11213835201691409920)
XLA Ops:
  0.0 0.5 %collective-permute-start.6 = (bf16[128,7168]{1,0:T(8,128)(2,1)}, bf16[128,7168]{1,0:T(8,128)(2,1)S(1)}, u32[]{:S(2)}, u32[]{:S(2)}) collective-permute-start(bf16[128,7168]{1,0:T(8,128)(2,1)} %bitcast.10), channel_id=1, source_target_pairs={{0,4},{4,0},{8,12},{12,8},{16,20},{20,16},{24,28},{28,24},{1,5},{5... | collective-permute-start | bytes 5505032 | tf_op jit(solution)/shard_map/ppermute | solution.py:81
  0.5 0.0 slice-start
  0.5 0.0 slice-start.1
  0.5 0.0 slice-start.2
  0.5 0.0 slice-start.3
  0.5 1.4 %prepare.1 = (bf16[4,7168]{1,0:T(4,128)(2,1)S(1)}, bf16[4,7168]{1,0:T(4,128)(2,1)S(1)}, bf16[4,7168]{1,0:T(4,128)(2,1)S(1)}, bf16[4,7168]{1,0:T(4,128)(2,1)S(1)}, f32[8,128]{1,0:T(8,128)S(1)}) custom-call(s32[1,4]{1,0:T(1,128)} %bitcast.16, bf16[4,7168]{1,0:T(4,128)(2,1)} %bitcast.14, f32[1,7168]{1,0:T(1,128)} %bitcast.15), custom_call_target="tpu_custom_call" | custom-call | flops 10000000000 | bytes 20000000 | tf_op jit(solution)/shard_map/prepare/pallas_call | solution.py:304
  1.9 2.6 %collective-permute-start = (bf16[4,7168]{1,0:T(4,128)(2,1)S(1)}, bf16[4,7168]{1,0:T(4,128)(2,1)S(1)}, u32[]{:S(2)}, u32[]{:S(2)}) collective-permute-start(bf16[4,7168]{1,0:T(4,128)(2,1)S(1)} %get-tuple-element.22), channel_id=1, source_target_pairs={{0,2},{1,3},{2,0},{3,1},{4,5},{5,4},{6,7},{7,6},{8,10},{9,11},{10,... | collective-permute-start | bytes 172040 | tf_op jit(solution)/shard_map/ppermute | solution.py:291
  4.5 1.5 %collective-permute-start.1 = (bf16[4,7168]{1,0:T(4,128)(2,1)S(1)}, bf16[4,7168]{1,0:T(4,128)(2,1)S(1)}, u32[]{:S(2)}, u32[]{:S(2)}) collective-permute-start(bf16[4,7168]{1,0:T(4,128)(2,1)S(1)} %get-tuple-element.23), channel_id=1, source_target_pairs={{0,1},{1,0},{2,3},{3,2},{4,6},{5,7},{6,4},{7,5},{8,9},{9,8},{10,11... | collective-permute-start | bytes 172040 | tf_op jit(solution)/shard_map/ppermute | solution.py:291
  5.9 0.1 collective-permute-start.2
  6.0 0.6 %collective-permute-done.refs_1_ = bf16[4,7168]{1,0:T(4,128)(2,1)S(1)} collective-permute-done((bf16[4,7168]{1,0:T(4,128)(2,1)S(1)}, bf16[4,7168]{1,0:T(4,128)(2,1)S(1)}, u32[]{:S(2)}, u32[]{:S(2)}) %collective-permute-start) | collective-permute-done | bytes 57376 | tf_op jit(solution)/shard_map/ppermute | solution.py:291
  6.6 2.2 %collective-permute-done.1.refs_2_ = bf16[4,7168]{1,0:T(4,128)(2,1)S(1)} collective-permute-done((bf16[4,7168]{1,0:T(4,128)(2,1)S(1)}, bf16[4,7168]{1,0:T(4,128)(2,1)S(1)}, u32[]{:S(2)}, u32[]{:S(2)}) %collective-permute-start.1) | collective-permute-done | bytes 57376 | tf_op jit(solution)/shard_map/ppermute | solution.py:291
  8.9 2.2 %collective-permute-done.2.refs_3_ = bf16[4,7168]{1,0:T(4,128)(2,1)S(1)} collective-permute-done((bf16[4,7168]{1,0:T(4,128)(2,1)S(1)}, bf16[4,7168]{1,0:T(4,128)(2,1)S(1)}, u32[]{:S(2)}, u32[]{:S(2)}) %collective-permute-start.2) | collective-permute-done | bytes 57376 | tf_op jit(solution)/shard_map/ppermute | solution.py:291
  11.0 0.0 slice-done
  11.0 0.0 slice-done.1
  11.0 0.0 slice-done.2
  11.0 0.0 slice-done.3
  11.1 0.0 copy-start
  11.1 3.9 %activate.1.refs_0_ = bf16[16,512]{1,0:T(8,128)(2,1)S(1)} custom-call(bf16[2,512,7168]{2,1,0:T(8,128)(2,1)S(1)} %bitcast.9, f32[8,128]{1,0:T(8,128)S(1)} %get-tuple-element.20.code_ref.after, bf16[4,7168]{1,0:T(4,128)(2,1)S(1)} %get-tuple-element.21.refs_0_, bf16[4,7168]{1,0:T(4,128)(2,1)S(1)} %collective-permute-done.refs_1_, ...), custom_call_target="tpu_custom_call" | custom-call | tf_op jit(solution)/shard_map/activate/pallas_call | solution.py:333
  15.0 3.6 %collective-permute-start.5 = (bf16[16,512]{1,0:T(8,128)(2,1)S(1)}, bf16[16,512]{1,0:T(8,128)(2,1)S(1)}, u32[]{:S(2)}, u32[]{:S(2)}) collective-permute-start(bf16[16,512]{1,0:T(8,128)(2,1)S(1)} %activate.1.refs_0_), channel_id=1, source_target_pairs={{0,24},{1,25},{2,26},{3,27},{4,28},{5,29},{6,30},{7,31},{8,16},{9,... | collective-permute-start | bytes 49160 | tf_op jit(solution)/shard_map/ppermute | solution.py:291
  18.6 0.0 collective-permute-start.4
  18.6 0.8 %collective-permute-start.3 = (bf16[16,512]{1,0:T(8,128)(2,1)S(1)}, bf16[16,512]{1,0:T(8,128)(2,1)S(1)}, u32[]{:S(2)}, u32[]{:S(2)}) collective-permute-start(bf16[16,512]{1,0:T(8,128)(2,1)S(1)} %activate.1.refs_0_), channel_id=1, source_target_pairs={{0,8},{1,9},{2,10},{3,11},{4,12},{5,13},{6,14},{7,15},{8,0},{9,1},... | collective-permute-start | bytes 49160 | tf_op jit(solution)/shard_map/ppermute | solution.py:291
  19.4 0.7 %flag.1 = (f32[8,128]{1,0:T(8,128)S(1)}, bf16[4,192,16]{2,1,0:T(8,128)(2,1)S(1)}) custom-call(s32[1,8]{1,0:T(1,128)} %bitcast.13, f32[8,128]{1,0:T(8,128)S(1)} %get-tuple-element.20.code_ref.after), custom_call_target="tpu_custom_call" | custom-call | tf_op jit(solution)/shard_map/flag/pallas_call | solution.py:321
  20.1 0.5 %collective-permute-done.5.refs_3_ = bf16[16,512]{1,0:T(8,128)(2,1)S(1)} collective-permute-done((bf16[16,512]{1,0:T(8,128)(2,1)S(1)}, bf16[16,512]{1,0:T(8,128)(2,1)S(1)}, u32[]{:S(2)}, u32[]{:S(2)}) %collective-permute-start.5) | collective-permute-done | bytes 16416 | tf_op jit(solution)/shard_map/ppermute | solution.py:291
  20.5 2.7 %collective-permute-done.4.refs_2_ = bf16[16,512]{1,0:T(8,128)(2,1)S(1)} collective-permute-done((bf16[16,512]{1,0:T(8,128)(2,1)S(1)}, bf16[16,512]{1,0:T(8,128)(2,1)S(1)}, u32[]{:S(2)}, u32[]{:S(2)}) %collective-permute-start.4) | collective-permute-done | bytes 16416 | tf_op jit(solution)/shard_map/ppermute | solution.py:291
  23.2 0.0 collective-permute-done.3.refs_1_
  23.2 0.0 collective-permute-done.6.other
  23.2 0.0 copy-done
  23.2 0.0 copy-start.1
  23.2 1.1 %down.1 = (bf16[24,3584]{1,0:T(8,128)(2,1)S(1)}, bf16[24,3584]{1,0:T(8,128)(2,1)S(1)}, bf16[24,3584]{1,0:T(8,128)(2,1)S(1)}, bf16[24,3584]{1,0:T(8,128)(2,1)S(1)}) custom-call(bf16[128,7168]{1,0:T(8,128)(2,1)S(1)} %bitcast.11, bf16[128,7168]{1,0:T(8,128)(2,1)S(1)} %collective-permute-done.6.other, f32[8,128]{1,0:T(8,128)S(1)} %get-tuple-element.25.flags, ...), custom_call_target="tpu_custom_call" | custom-call | tf_op jit(solution)/shard_map/down/pallas_call | solution.py:344
  24.3 0.6 %collective-permute-start.7 = (bf16[24,3584]{1,0:T(8,128)(2,1)S(1)}, bf16[24,3584]{1,0:T(8,128)(2,1)S(1)}, u32[]{:S(2)}, u32[]{:S(2)}) collective-permute-start(bf16[24,3584]{1,0:T(8,128)(2,1)S(1)} %get-tuple-element.28), channel_id=1, source_target_pairs={{0,2},{1,3},{2,0},{3,1},{4,5},{5,4},{6,7},{7,6},{8,10},{9,11},{10,... | collective-permute-start | bytes 516104 | tf_op jit(solution)/shard_map/ppermute | solution.py:291
  24.9 0.7 %collective-permute-start.8 = (bf16[24,3584]{1,0:T(8,128)(2,1)S(1)}, bf16[24,3584]{1,0:T(8,128)(2,1)S(1)}, u32[]{:S(2)}, u32[]{:S(2)}) collective-permute-start(bf16[24,3584]{1,0:T(8,128)(2,1)S(1)} %get-tuple-element.29), channel_id=1, source_target_pairs={{0,1},{1,0},{2,3},{3,2},{4,6},{5,7},{6,4},{7,5},{8,9},{9,8},{10,11... | collective-permute-start | bytes 516104 | tf_op jit(solution)/shard_map/ppermute | solution.py:291
  25.6 2.3 %collective-permute-start.9 = (bf16[24,3584]{1,0:T(8,128)(2,1)S(1)}, bf16[24,3584]{1,0:T(8,128)(2,1)S(1)}, u32[]{:S(2)}, u32[]{:S(2)}) collective-permute-start(bf16[24,3584]{1,0:T(8,128)(2,1)S(1)} %get-tuple-element.30), channel_id=1, source_target_pairs={{0,3},{1,2},{2,1},{3,0},{4,7},{5,6},{6,5},{7,4},{8,11},{9,10},{10,... | collective-permute-start | bytes 516104 | tf_op jit(solution)/shard_map/ppermute | solution.py:291
  27.9 0.1 place.1.placing
  28.0 2.3 %collective-permute-done.7.refs_1_ = bf16[24,3584]{1,0:T(8,128)(2,1)S(1)} collective-permute-done((bf16[24,3584]{1,0:T(8,128)(2,1)S(1)}, bf16[24,3584]{1,0:T(8,128)(2,1)S(1)}, u32[]{:S(2)}, u32[]{:S(2)}) %collective-permute-start.7) | collective-permute-done | bytes 172064 | tf_op jit(solution)/shard_map/ppermute | solution.py:291
  30.3 0.0 collective-permute-done.8.refs_2_
  30.3 2.8 %collective-permute-done.9.refs_3_ = bf16[24,3584]{1,0:T(8,128)(2,1)S(1)} collective-permute-done((bf16[24,3584]{1,0:T(8,128)(2,1)S(1)}, bf16[24,3584]{1,0:T(8,128)(2,1)S(1)}, u32[]{:S(2)}, u32[]{:S(2)}) %collective-permute-start.9) | collective-permute-done | bytes 172064 | tf_op jit(solution)/shard_map/ppermute | solution.py:291
  33.1 0.4 combine.1
  33.5 0.1 collective-permute-start.10
  33.6 2.1 %collective-permute-start.11 = (bf16[4,7168]{1,0:T(4,128)(2,1)S(1)}, bf16[4,7168]{1,0:T(4,128)(2,1)S(1)}, u32[]{:S(2)}, u32[]{:S(2)}) collective-permute-start(bf16[4,7168]{1,0:T(4,128)(2,1)S(1)} %get-tuple-element.33), channel_id=1, source_target_pairs={{0,16},{1,17},{2,18},{3,19},{4,20},{5,21},{6,22},{7,23},{8,24},{9,... | collective-permute-start | bytes 172040 | tf_op jit(solution)/shard_map/ppermute | solution.py:291
  35.7 2.3 %collective-permute-start.12 = (bf16[4,7168]{1,0:T(4,128)(2,1)S(1)}, bf16[4,7168]{1,0:T(4,128)(2,1)S(1)}, u32[]{:S(2)}, u32[]{:S(2)}) collective-permute-start(bf16[4,7168]{1,0:T(4,128)(2,1)S(1)} %get-tuple-element.34), channel_id=1, source_target_pairs={{0,24},{1,25},{2,26},{3,27},{4,28},{5,29},{6,30},{7,31},{8,16},{9,... | collective-permute-start | bytes 172040 | tf_op jit(solution)/shard_map/ppermute | solution.py:291
  37.9 0.0 collective-permute-done.10
  37.9 0.8 %collective-permute-done.11 = bf16[4,7168]{1,0:T(4,128)(2,1)S(1)} collective-permute-done((bf16[4,7168]{1,0:T(4,128)(2,1)S(1)}, bf16[4,7168]{1,0:T(4,128)(2,1)S(1)}, u32[]{:S(2)}, u32[]{:S(2)}) %collective-permute-start.11) | collective-permute-done | bytes 57376 | tf_op jit(solution)/shard_map/ppermute | solution.py:291
  38.7 3.0 %collective-permute-done.12 = bf16[4,7168]{1,0:T(4,128)(2,1)S(1)} collective-permute-done((bf16[4,7168]{1,0:T(4,128)(2,1)S(1)}, bf16[4,7168]{1,0:T(4,128)(2,1)S(1)}, u32[]{:S(2)}, u32[]{:S(2)}) %collective-permute-start.12) | collective-permute-done | bytes 57376 | tf_op jit(solution)/shard_map/ppermute | solution.py:291
  41.7 0.0 copy-done.1
  41.7 0.7 %fusion = bf16[1,4,7168]{2,1,0:T(4,128)(2,1)} fusion(bf16[4,7168]{1,0:T(4,128)(2,1)S(1)} %collective-permute-done.12, bf16[4,7168]{1,0:T(4,128)(2,1)S(1)} %collective-permute-done.11, bf16[4,7168]{1,0:T(4,128)(2,1)S(1)} %collective-permute-done.10, bf16[4,7168]{1,0:T(4,128)(2,1)S(1)} %get-tuple-element.31, f32[4]{0:T(128)S(1)} %bitcast.12), kind=kLoop, calls=%fused_computation.1 | loop fusion | flops 258048 | bytes 286736 | tf_op jit(solution)/shard_map/reshape | solution.py:374
  (1 shorter events, 0.0 us)
Async XLA Ops:
  0.0 23.2 %collective-permute-start.6 = (bf16[128,7168]{1,0:T(8,128)(2,1)}, bf16[128,7168]{1,0:T(8,128)(2,1)S(1)}, u32[]{:S(2)}, u32[]{:S(2)}) collective-permute-start(bf16[128,7168]{1,0:T(8,128)(2,1)} %bitcast.10), channel_id=1, source_target_pairs={{0,4},{4,0},{8,12},{12,8},{16,20},{20,16},{24,28},{28,24},{1,5},{5... | collective-permute-start | bytes 5505032 | tf_op jit(solution)/shard_map/ppermute | solution.py:81
  0.5 10.5 %slice-start = ((s8[14680064]{0:T(1024)(128)(4,1)}), s8[4194304]{0:T(1024)(128)(4,1)S(1)}, s32[]{:S(2)}) async-start(s8[14680064]{0:T(1024)(128)(4,1)} %bitcast.8), calls=%async_computation | async-start | bytes 8388608
  0.5 10.5 %slice-start.1 = ((s8[14680064]{0:T(1024)(128)(4,1)}), s8[4194304]{0:T(1024)(128)(4,1)S(1)}, s32[]{:S(2)}) async-start(s8[14680064]{0:T(1024)(128)(4,1)} %bitcast.8), calls=%async_computation.1 | async-start | bytes 8388608
  0.5 10.5 %slice-start.2 = ((s8[14680064]{0:T(1024)(128)(4,1)}), s8[4194304]{0:T(1024)(128)(4,1)S(1)}, s32[]{:S(2)}) async-start(s8[14680064]{0:T(1024)(128)(4,1)} %bitcast.8), calls=%async_computation.2 | async-start | bytes 8388608
  0.5 10.5 %slice-start.3 = ((s8[14680064]{0:T(1024)(128)(4,1)}), s8[2097152]{0:T(1024)(128)(4,1)S(1)}, s32[]{:S(2)}) async-start(s8[14680064]{0:T(1024)(128)(4,1)} %bitcast.8), calls=%async_computation.3 | async-start | bytes 4194304
  1.9 4.7 %collective-permute-start = (bf16[4,7168]{1,0:T(4,128)(2,1)S(1)}, bf16[4,7168]{1,0:T(4,128)(2,1)S(1)}, u32[]{:S(2)}, u32[]{:S(2)}) collective-permute-start(bf16[4,7168]{1,0:T(4,128)(2,1)S(1)} %get-tuple-element.22), channel_id=1, source_target_pairs={{0,2},{1,3},{2,0},{3,1},{4,5},{5,4},{6,7},{7,6},{8,10},{9,11},{10,... | collective-permute-start | bytes 172040 | tf_op jit(solution)/shard_map/ppermute | solution.py:291
  4.5 4.4 %collective-permute-start.1 = (bf16[4,7168]{1,0:T(4,128)(2,1)S(1)}, bf16[4,7168]{1,0:T(4,128)(2,1)S(1)}, u32[]{:S(2)}, u32[]{:S(2)}) collective-permute-start(bf16[4,7168]{1,0:T(4,128)(2,1)S(1)} %get-tuple-element.23), channel_id=1, source_target_pairs={{0,1},{1,0},{2,3},{3,2},{4,6},{5,7},{6,4},{7,5},{8,9},{9,8},{10,11... | collective-permute-start | bytes 172040 | tf_op jit(solution)/shard_map/ppermute | solution.py:291
  5.9 5.1 %collective-permute-start.2 = (bf16[4,7168]{1,0:T(4,128)(2,1)S(1)}, bf16[4,7168]{1,0:T(4,128)(2,1)S(1)}, u32[]{:S(2)}, u32[]{:S(2)}) collective-permute-start(bf16[4,7168]{1,0:T(4,128)(2,1)S(1)} %get-tuple-element.24), channel_id=1, source_target_pairs={{0,3},{1,2},{2,1},{3,0},{4,7},{5,6},{6,5},{7,4},{8,11},{9,10},{10,... | collective-permute-start | bytes 172040 | tf_op jit(solution)/shard_map/ppermute | solution.py:291
  11.1 12.2 %copy-start = (bf16[1,128,7168]{2,1,0:T(8,128)(2,1)S(1)}, bf16[1,128,7168]{2,1,0:T(8,128)(2,1)}, u32[]{:S(2)}) copy-start(bf16[1,128,7168]{2,1,0:T(8,128)(2,1)} %param.12) | copy-start | bytes 5505028
  15.0 5.5 %collective-permute-start.5 = (bf16[16,512]{1,0:T(8,128)(2,1)S(1)}, bf16[16,512]{1,0:T(8,128)(2,1)S(1)}, u32[]{:S(2)}, u32[]{:S(2)}) collective-permute-start(bf16[16,512]{1,0:T(8,128)(2,1)S(1)} %activate.1.refs_0_), channel_id=1, source_target_pairs={{0,24},{1,25},{2,26},{3,27},{4,28},{5,29},{6,30},{7,31},{8,16},{9,... | collective-permute-start | bytes 49160 | tf_op jit(solution)/shard_map/ppermute | solution.py:291
  18.6 4.6 %collective-permute-start.4 = (bf16[16,512]{1,0:T(8,128)(2,1)S(1)}, bf16[16,512]{1,0:T(8,128)(2,1)S(1)}, u32[]{:S(2)}, u32[]{:S(2)}) collective-permute-start(bf16[16,512]{1,0:T(8,128)(2,1)S(1)} %activate.1.refs_0_), channel_id=1, source_target_pairs={{0,16},{1,17},{2,18},{3,19},{4,20},{5,21},{6,22},{7,23},{8,24},{9,... | collective-permute-start | bytes 49160 | tf_op jit(solution)/shard_map/ppermute | solution.py:291
  18.6 4.6 %collective-permute-start.3 = (bf16[16,512]{1,0:T(8,128)(2,1)S(1)}, bf16[16,512]{1,0:T(8,128)(2,1)S(1)}, u32[]{:S(2)}, u32[]{:S(2)}) collective-permute-start(bf16[16,512]{1,0:T(8,128)(2,1)S(1)} %activate.1.refs_0_), channel_id=1, source_target_pairs={{0,8},{1,9},{2,10},{3,11},{4,12},{5,13},{6,14},{7,15},{8,0},{9,1},... | collective-permute-start | bytes 49160 | tf_op jit(solution)/shard_map/ppermute | solution.py:291
  23.2 18.5 %copy-start.1 = (f32[1,4]{1,0:T(1,128)S(1)}, f32[1,4]{1,0:T(1,128)}, u32[]{:S(2)}) copy-start(f32[1,4]{1,0:T(1,128)} %param.10) | copy-start | bytes 52
  24.3 6.0 %collective-permute-start.7 = (bf16[24,3584]{1,0:T(8,128)(2,1)S(1)}, bf16[24,3584]{1,0:T(8,128)(2,1)S(1)}, u32[]{:S(2)}, u32[]{:S(2)}) collective-permute-start(bf16[24,3584]{1,0:T(8,128)(2,1)S(1)} %get-tuple-element.28), channel_id=1, source_target_pairs={{0,2},{1,3},{2,0},{3,1},{4,5},{5,4},{6,7},{7,6},{8,10},{9,11},{10,... | collective-permute-start | bytes 516104 | tf_op jit(solution)/shard_map/ppermute | solution.py:291
  24.9 5.4 %collective-permute-start.8 = (bf16[24,3584]{1,0:T(8,128)(2,1)S(1)}, bf16[24,3584]{1,0:T(8,128)(2,1)S(1)}, u32[]{:S(2)}, u32[]{:S(2)}) collective-permute-start(bf16[24,3584]{1,0:T(8,128)(2,1)S(1)} %get-tuple-element.29), channel_id=1, source_target_pairs={{0,1},{1,0},{2,3},{3,2},{4,6},{5,7},{6,4},{7,5},{8,9},{9,8},{10,11... | collective-permute-start | bytes 516104 | tf_op jit(solution)/shard_map/ppermute | solution.py:291
  25.6 7.5 %collective-permute-start.9 = (bf16[24,3584]{1,0:T(8,128)(2,1)S(1)}, bf16[24,3584]{1,0:T(8,128)(2,1)S(1)}, u32[]{:S(2)}, u32[]{:S(2)}) collective-permute-start(bf16[24,3584]{1,0:T(8,128)(2,1)S(1)} %get-tuple-element.30), channel_id=1, source_target_pairs={{0,3},{1,2},{2,1},{3,0},{4,7},{5,6},{6,5},{7,4},{8,11},{9,10},{10,... | collective-permute-start | bytes 516104 | tf_op jit(solution)/shard_map/ppermute | solution.py:291
  33.5 4.5 %collective-permute-start.10 = (bf16[4,7168]{1,0:T(4,128)(2,1)S(1)}, bf16[4,7168]{1,0:T(4,128)(2,1)S(1)}, u32[]{:S(2)}, u32[]{:S(2)}) collective-permute-start(bf16[4,7168]{1,0:T(4,128)(2,1)S(1)} %get-tuple-element.32), channel_id=1, source_target_pairs={{0,8},{1,9},{2,10},{3,11},{4,12},{5,13},{6,14},{7,15},{8,0},{9,1},... | collective-permute-start | bytes 172040 | tf_op jit(solution)/shard_map/ppermute | solution.py:291
  33.6 5.1 %collective-permute-start.11 = (bf16[4,7168]{1,0:T(4,128)(2,1)S(1)}, bf16[4,7168]{1,0:T(4,128)(2,1)S(1)}, u32[]{:S(2)}, u32[]{:S(2)}) collective-permute-start(bf16[4,7168]{1,0:T(4,128)(2,1)S(1)} %get-tuple-element.33), channel_id=1, source_target_pairs={{0,16},{1,17},{2,18},{3,19},{4,20},{5,21},{6,22},{7,23},{8,24},{9,... | collective-permute-start | bytes 172040 | tf_op jit(solution)/shard_map/ppermute | solution.py:291
  35.7 6.1 %collective-permute-start.12 = (bf16[4,7168]{1,0:T(4,128)(2,1)S(1)}, bf16[4,7168]{1,0:T(4,128)(2,1)S(1)}, u32[]{:S(2)}, u32[]{:S(2)}) collective-permute-start(bf16[4,7168]{1,0:T(4,128)(2,1)S(1)} %get-tuple-element.34), channel_id=1, source_target_pairs={{0,24},{1,25},{2,26},{3,27},{4,28},{5,29},{6,30},{7,31},{8,16},{9,... | collective-permute-start | bytes 172040 | tf_op jit(solution)/shard_map/ppermute | solution.py:291

commit v2 on v0

--- a/solution.py
+++ b/solution.py
@@ -263,17 +263,10 @@
             ].astype(outs[chip].dtype)
 
 
-def exchange(values, axis):
-    groups, devices = lax.axis_size("grp"), lax.axis_size("exp")
+def exchange(values, axis, unit):
     moved = [values[0]]
     for bits in range(1, len(values)):
-        group_bits, bits_along = (1, bits) if axis == "exp" else (PAIR * bits + 1, 0)
-        pairs = [
-            (group * devices + index, (group ^ group_bits) * devices + (index ^ bits_along))
-            for group in range(groups)
-            for index in range(devices)
-        ]
-        moved.append(lax.ppermute(values[bits], ("grp", "exp"), pairs))
+        moved.append(swap(values[bits], axis, bits * unit))
     return moved
 
 
@@ -301,7 +294,7 @@
         cost_estimate=pl.CostEstimate(flops=10**10, transcendentals=0, bytes_accessed=2 * 10**7),
         name="prepare",
     )(*in_hbm(route.reshape(1, row_count), rows, norm_gain.reshape(1, width)))
-    arrived = exchange([packed[bits // shards] for bits in range(devices)], "exp")
+    arrived = exchange([packed[bits // shards] for bits in range(devices)], "exp", 1)
     other_piece = swap(own_piece, "grp", 1)
     flags, spots = pl.pallas_call(
         functools.partial(flag_body, chips, row_count),
@@ -324,7 +317,7 @@
         compiler_params=limit(20),
         name="activate",
     )(resident, *held(code, *arrived))
-    acts = exchange([act] * chips, "grp")
+    acts = exchange([act] * chips, "grp", PAIR)
     half_block = pltpu.VMEM((block, half), jnp.bfloat16)
     partials = pl.pallas_call(
         functools.partial(down_body, devices, chips),
@@ -334,7 +327,7 @@
         compiler_params=limit(12),
         name="down",
     )(*held(own_piece, other_piece, flags, spots, *acts))
-    returned = exchange(partials, "exp")
+    returned = exchange(partials, "exp", 1)
     placing = pl.pallas_call(
         functools.partial(place_body, chips, shards, row_count, block),
         out_shape=pltpu.VMEM((2 * E_WIN, chips * row_count, CODE), jnp.bfloat16),
@@ -353,7 +346,7 @@
         name="combine",
     )(*held(placing, *returned))
     combined = 0.0
-    for share in exchange(sums, "grp"):
+    for share in exchange(sums, "grp", PAIR):
         combined = combined + share.astype(jnp.float32)
     result = (combined * route_weight[0][:, None]).astype(jnp.bfloat16)
     return result.reshape(1, row_count, width)

time: 42.9 us -> 43.3 us (level)
  starting transfers between devices: 15.4 us -> 17 us
  waiting for transfers between devices: 19 us -> 17.8 us
    ppermute x12 -> x0, waiting for transfers between devices: 19 us -> none  [exchange(): moved.append(lax.ppermute(values[bits], ('grp', 'exp'), pairs))]
    ppermute x1 -> x13, waiting for transfers between devices: 0.01 us -> 17.8 us  [swap(): return lax.ppermute(value, axis, [(i, i ^ bits) for i in range(size)])]
    ppermute x1 -> x13, starting transfers between devices: 0.49 us -> 17 us  [swap(): return lax.ppermute(value, axis, [(i, i ^ bits) for i in range(size)])]
    ppermute x12 -> x0, starting transfers between devices: 14.9 us -> none  [exchange(): moved.append(lax.ppermute(values[bits], ('grp', 'exp'), pairs))]
  transfers between devices with their start and end apart: 13 -> 13, of which waited for: 10 -> 9; matrix products, arithmetic and copies ran while one was open for 0% -> 0% of each run, Pallas kernels for 14% -> 14%
where the time goes in v2:
time: 43.3 us; the launch traced here: 43.2 us
  waiting for transfers between devices  17.8 us (41%)
  starting transfers between devices  17 us (39%)
  Pallas kernels  7.51 us (17%)
  other arithmetic  0.71 us (2%)
    ppermute x13, waiting for transfers between devices, swap(): return lax.ppermute(value, axis, [(i, i ^ bits) for i in range(size)])  17.8 us
    ppermute x13, starting transfers between devices, swap(): return lax.ppermute(value, axis, [(i, i ^ bits) for i in range(size)])  17 us
    pallas_call x1, Pallas kernels, move_rows(): pl.pallas_call(functools.partial(activate_body, devices), out_shape=pltpu...  3.91 us
    pallas_call x1, Pallas kernels, move_rows(): pl.pallas_call(functools.partial(prepare_body, shards), out_shape=[row_bl...  1.35 us
    pallas_call x1, Pallas kernels, move_rows(): pl.pallas_call(functools.partial(down_body, devices, chips), out_shape=[h...  1.07 us
  transfers between devices with their start and end apart: 13, of which 9 were waited for; matrix products, arithmetic and copies ran while one was open for 0% of the time, Pallas kernels for 14%

profile of v2, /device:TPU:0, one launch (start us, length us, event | category | flops | bytes accessed | tf_op | source)
XLA Modules:
  0.0 43.2 jit_solution(9770215840379510788)
XLA Ops:
  0.0 0.5 %collective-permute-start.6 = (bf16[128,7168]{1,0:T(8,128)(2,1)}, bf16[128,7168]{1,0:T(8,128)(2,1)S(1)}, u32[]{:S(2)}, u32[]{:S(2)}) collective-permute-start(bf16[128,7168]{1,0:T(8,128)(2,1)} %bitcast.10), channel_id=1, source_target_pairs={{0,4},{4,0},{8,12},{12,8},{16,20},{20,16},{24,28},{28,24},{1,5},{5... | collective-permute-start | bytes 5505032 | tf_op jit(solution)/shard_map/ppermute | solution.py:81
  0.5 0.0 slice-start
  0.5 0.0 slice-start.1
  0.5 0.0 slice-start.2
  0.5 0.0 slice-start.3
  0.5 1.4 %prepare.1 = (bf16[4,7168]{1,0:T(4,128)(2,1)S(1)}, bf16[4,7168]{1,0:T(4,128)(2,1)S(1)}, f32[8,128]{1,0:T(8,128)S(1)}) custom-call(s32[1,4]{1,0:T(1,128)} %bitcast.16, bf16[4,7168]{1,0:T(4,128)(2,1)} %bitcast.14, f32[1,7168]{1,0:T(1,128)} %bitcast.15), custom_call_target="tpu_custom_call" | custom-call | flops 10000000000 | bytes 20000000 | tf_op jit(solution)/shard_map/prepare/pallas_call | solution.py:282
  1.9 2.6 %collective-permute-start = (bf16[4,7168]{1,0:T(4,128)(2,1)S(1)}, bf16[4,7168]{1,0:T(4,128)(2,1)S(1)}, u32[]{:S(2)}, u32[]{:S(2)}) collective-permute-start(bf16[4,7168]{1,0:T(4,128)(2,1)S(1)} %get-tuple-element.19.refs_0_), channel_id=1, source_target_pairs={{0,1},{1,0},{2,3},{3,2},{4,5},{5,4},{6,7},{7,6},{8,9},{9,8},{10,11... | collective-permute-start | bytes 172040 | tf_op jit(solution)/shard_map/ppermute | solution.py:81
  4.4 1.5 %collective-permute-start.2 = (bf16[4,7168]{1,0:T(4,128)(2,1)S(1)}, bf16[4,7168]{1,0:T(4,128)(2,1)S(1)}, u32[]{:S(2)}, u32[]{:S(2)}) collective-permute-start(bf16[4,7168]{1,0:T(4,128)(2,1)S(1)} %get-tuple-element.20), channel_id=1, source_target_pairs={{0,3},{1,2},{2,1},{3,0},{4,7},{5,6},{6,5},{7,4},{8,11},{9,10},{10,... | collective-permute-start | bytes 172040 | tf_op jit(solution)/shard_map/ppermute | solution.py:81
  5.9 0.1 collective-permute-start.1
  6.0 1.0 %collective-permute-done.refs_1_ = bf16[4,7168]{1,0:T(4,128)(2,1)S(1)} collective-permute-done((bf16[4,7168]{1,0:T(4,128)(2,1)S(1)}, bf16[4,7168]{1,0:T(4,128)(2,1)S(1)}, u32[]{:S(2)}, u32[]{:S(2)}) %collective-permute-start) | collective-permute-done | bytes 57376 | tf_op jit(solution)/shard_map/ppermute | solution.py:81
  7.0 2.5 %collective-permute-done.2.refs_3_ = bf16[4,7168]{1,0:T(4,128)(2,1)S(1)} collective-permute-done((bf16[4,7168]{1,0:T(4,128)(2,1)S(1)}, bf16[4,7168]{1,0:T(4,128)(2,1)S(1)}, u32[]{:S(2)}, u32[]{:S(2)}) %collective-permute-start.2) | collective-permute-done | bytes 57376 | tf_op jit(solution)/shard_map/ppermute | solution.py:81
  9.5 1.1 %collective-permute-done.1.refs_2_ = bf16[4,7168]{1,0:T(4,128)(2,1)S(1)} collective-permute-done((bf16[4,7168]{1,0:T(4,128)(2,1)S(1)}, bf16[4,7168]{1,0:T(4,128)(2,1)S(1)}, u32[]{:S(2)}, u32[]{:S(2)}) %collective-permute-start.1) | collective-permute-done | bytes 57376 | tf_op jit(solution)/shard_map/ppermute | solution.py:81
  10.7 0.0 slice-done
  10.7 0.0 slice-done.1
  10.7 0.0 slice-done.2
  10.7 0.0 slice-done.3
  10.7 0.0 copy-start
  10.7 3.9 %activate.1.refs_0_ = bf16[16,512]{1,0:T(8,128)(2,1)S(1)} custom-call(bf16[2,512,7168]{2,1,0:T(8,128)(2,1)S(1)} %bitcast.9, f32[8,128]{1,0:T(8,128)S(1)} %get-tuple-element.18.code_ref.after, bf16[4,7168]{1,0:T(4,128)(2,1)S(1)} %get-tuple-element.19.refs_0_, bf16[4,7168]{1,0:T(4,128)(2,1)S(1)} %collective-permute-done.refs_1_, ...), custom_call_target="tpu_custom_call" | custom-call | tf_op jit(solution)/shard_map/activate/pallas_call | solution.py:311
  14.6 3.6 %collective-permute-start.5 = (bf16[16,512]{1,0:T(8,128)(2,1)S(1)}, bf16[16,512]{1,0:T(8,128)(2,1)S(1)}, u32[]{:S(2)}, u32[]{:S(2)}) collective-permute-start(bf16[16,512]{1,0:T(8,128)(2,1)S(1)} %activate.1.refs_0_), channel_id=1, source_target_pairs={{0,24},{4,28},{8,16},{12,20},{16,8},{20,12},{24,0},{28,4},{1,25},{... | collective-permute-start | bytes 49160 | tf_op jit(solution)/shard_map/ppermute | solution.py:81
  18.2 0.0 collective-permute-start.4
  18.2 0.8 %collective-permute-start.3 = (bf16[16,512]{1,0:T(8,128)(2,1)S(1)}, bf16[16,512]{1,0:T(8,128)(2,1)S(1)}, u32[]{:S(2)}, u32[]{:S(2)}) collective-permute-start(bf16[16,512]{1,0:T(8,128)(2,1)S(1)} %activate.1.refs_0_), channel_id=1, source_target_pairs={{0,8},{4,12},{8,0},{12,4},{16,24},{20,28},{24,16},{28,20},{1,9},{5... | collective-permute-start | bytes 49160 | tf_op jit(solution)/shard_map/ppermute | solution.py:81
  19.0 0.7 %flag.1 = (f32[8,128]{1,0:T(8,128)S(1)}, bf16[4,192,16]{2,1,0:T(8,128)(2,1)S(1)}) custom-call(s32[1,8]{1,0:T(1,128)} %bitcast.13, f32[8,128]{1,0:T(8,128)S(1)} %get-tuple-element.18.code_ref.after), custom_call_target="tpu_custom_call" | custom-call | tf_op jit(solution)/shard_map/flag/pallas_call | solution.py:299
  19.7 0.5 %collective-permute-done.5.refs_3_ = bf16[16,512]{1,0:T(8,128)(2,1)S(1)} collective-permute-done((bf16[16,512]{1,0:T(8,128)(2,1)S(1)}, bf16[16,512]{1,0:T(8,128)(2,1)S(1)}, u32[]{:S(2)}, u32[]{:S(2)}) %collective-permute-start.5) | collective-permute-done | bytes 16416 | tf_op jit(solution)/shard_map/ppermute | solution.py:81
  20.2 2.7 %collective-permute-done.4.refs_2_ = bf16[16,512]{1,0:T(8,128)(2,1)S(1)} collective-permute-done((bf16[16,512]{1,0:T(8,128)(2,1)S(1)}, bf16[16,512]{1,0:T(8,128)(2,1)S(1)}, u32[]{:S(2)}, u32[]{:S(2)}) %collective-permute-start.4) | collective-permute-done | bytes 16416 | tf_op jit(solution)/shard_map/ppermute | solution.py:81
  22.9 0.0 collective-permute-done.3.refs_1_
  22.9 0.0 collective-permute-done.6.other
  22.9 0.0 copy-done
  22.9 0.0 copy-start.1
  22.9 1.1 %down.1 = (bf16[24,3584]{1,0:T(8,128)(2,1)S(1)}, bf16[24,3584]{1,0:T(8,128)(2,1)S(1)}, bf16[24,3584]{1,0:T(8,128)(2,1)S(1)}, bf16[24,3584]{1,0:T(8,128)(2,1)S(1)}) custom-call(bf16[128,7168]{1,0:T(8,128)(2,1)S(1)} %bitcast.11, bf16[128,7168]{1,0:T(8,128)(2,1)S(1)} %collective-permute-done.6.other, f32[8,128]{1,0:T(8,128)S(1)} %get-tuple-element.21.flags, ...), custom_call_target="tpu_custom_call" | custom-call | tf_op jit(solution)/shard_map/down/pallas_call | solution.py:322
  24.0 1.4 %collective-permute-start.7 = (bf16[24,3584]{1,0:T(8,128)(2,1)S(1)}, bf16[24,3584]{1,0:T(8,128)(2,1)S(1)}, u32[]{:S(2)}, u32[]{:S(2)}) collective-permute-start(bf16[24,3584]{1,0:T(8,128)(2,1)S(1)} %get-tuple-element.24), channel_id=1, source_target_pairs={{0,1},{1,0},{2,3},{3,2},{4,5},{5,4},{6,7},{7,6},{8,9},{9,8},{10,11... | collective-permute-start | bytes 516104 | tf_op jit(solution)/shard_map/ppermute | solution.py:81
  25.4 0.6 %collective-permute-start.8 = (bf16[24,3584]{1,0:T(8,128)(2,1)S(1)}, bf16[24,3584]{1,0:T(8,128)(2,1)S(1)}, u32[]{:S(2)}, u32[]{:S(2)}) collective-permute-start(bf16[24,3584]{1,0:T(8,128)(2,1)S(1)} %get-tuple-element.25), channel_id=1, source_target_pairs={{0,2},{1,3},{2,0},{3,1},{4,6},{5,7},{6,4},{7,5},{8,10},{9,11},{10,... | collective-permute-start | bytes 516104 | tf_op jit(solution)/shard_map/ppermute | solution.py:81
  26.0 1.5 %collective-permute-start.9 = (bf16[24,3584]{1,0:T(8,128)(2,1)S(1)}, bf16[24,3584]{1,0:T(8,128)(2,1)S(1)}, u32[]{:S(2)}, u32[]{:S(2)}) collective-permute-start(bf16[24,3584]{1,0:T(8,128)(2,1)S(1)} %get-tuple-element.26), channel_id=1, source_target_pairs={{0,3},{1,2},{2,1},{3,0},{4,7},{5,6},{6,5},{7,4},{8,11},{9,10},{10,... | collective-permute-start | bytes 516104 | tf_op jit(solution)/shard_map/ppermute | solution.py:81
  27.5 0.1 place.1.placing
  27.6 3.4 %collective-permute-done.7.refs_1_ = bf16[24,3584]{1,0:T(8,128)(2,1)S(1)} collective-permute-done((bf16[24,3584]{1,0:T(8,128)(2,1)S(1)}, bf16[24,3584]{1,0:T(8,128)(2,1)S(1)}, u32[]{:S(2)}, u32[]{:S(2)}) %collective-permute-start.7) | collective-permute-done | bytes 172064 | tf_op jit(solution)/shard_map/ppermute | solution.py:81
  31.1 2.5 %collective-permute-done.8.refs_2_ = bf16[24,3584]{1,0:T(8,128)(2,1)S(1)} collective-permute-done((bf16[24,3584]{1,0:T(8,128)(2,1)S(1)}, bf16[24,3584]{1,0:T(8,128)(2,1)S(1)}, u32[]{:S(2)}, u32[]{:S(2)}) %collective-permute-start.8) | collective-permute-done | bytes 172064 | tf_op jit(solution)/shard_map/ppermute | solution.py:81
  33.6 0.0 collective-permute-done.9.refs_3_
  33.6 0.4 combine.1
  34.0 0.1 collective-permute-start.10
  34.1 2.4 %collective-permute-start.11 = (bf16[4,7168]{1,0:T(4,128)(2,1)S(1)}, bf16[4,7168]{1,0:T(4,128)(2,1)S(1)}, u32[]{:S(2)}, u32[]{:S(2)}) collective-permute-start(bf16[4,7168]{1,0:T(4,128)(2,1)S(1)} %get-tuple-element.29), channel_id=1, source_target_pairs={{0,16},{4,20},{8,24},{12,28},{16,0},{20,4},{24,8},{28,12},{1,17},{... | collective-permute-start | bytes 172040 | tf_op jit(solution)/shard_map/ppermute | solution.py:81
  36.5 2.0 %collective-permute-start.12 = (bf16[4,7168]{1,0:T(4,128)(2,1)S(1)}, bf16[4,7168]{1,0:T(4,128)(2,1)S(1)}, u32[]{:S(2)}, u32[]{:S(2)}) collective-permute-start(bf16[4,7168]{1,0:T(4,128)(2,1)S(1)} %get-tuple-element.30), channel_id=1, source_target_pairs={{0,24},{4,28},{8,16},{12,20},{16,8},{20,12},{24,0},{28,4},{1,25},{... | collective-permute-start | bytes 172040 | tf_op jit(solution)/shard_map/ppermute | solution.py:81
  38.5 1.0 %collective-permute-done.10 = bf16[4,7168]{1,0:T(4,128)(2,1)S(1)} collective-permute-done((bf16[4,7168]{1,0:T(4,128)(2,1)S(1)}, bf16[4,7168]{1,0:T(4,128)(2,1)S(1)}, u32[]{:S(2)}, u32[]{:S(2)}) %collective-permute-start.10) | collective-permute-done | bytes 57376 | tf_op jit(solution)/shard_map/ppermute | solution.py:81
  39.5 0.0 collective-permute-done.11
  39.5 3.0 %collective-permute-done.12 = bf16[4,7168]{1,0:T(4,128)(2,1)S(1)} collective-permute-done((bf16[4,7168]{1,0:T(4,128)(2,1)S(1)}, bf16[4,7168]{1,0:T(4,128)(2,1)S(1)}, u32[]{:S(2)}, u32[]{:S(2)}) %collective-permute-start.12) | collective-permute-done | bytes 57376 | tf_op jit(solution)/shard_map/ppermute | solution.py:81
  42.5 0.0 copy-done.1
  42.5 0.7 %fusion = bf16[1,4,7168]{2,1,0:T(4,128)(2,1)} fusion(bf16[4,7168]{1,0:T(4,128)(2,1)S(1)} %collective-permute-done.12, bf16[4,7168]{1,0:T(4,128)(2,1)S(1)} %collective-permute-done.11, bf16[4,7168]{1,0:T(4,128)(2,1)S(1)} %collective-permute-done.10, bf16[4,7168]{1,0:T(4,128)(2,1)S(1)} %get-tuple-element.27, f32[4]{0:T(128)S(1)} %bitcast.12), kind=kLoop, calls=%fused_computation.1 | loop fusion | flops 258048 | bytes 286736 | tf_op jit(solution)/shard_map/reshape | solution.py:352
  (1 shorter events, 0.0 us)
Async XLA Ops:
  0.0 22.9 %collective-permute-start.6 = (bf16[128,7168]{1,0:T(8,128)(2,1)}, bf16[128,7168]{1,0:T(8,128)(2,1)S(1)}, u32[]{:S(2)}, u32[]{:S(2)}) collective-permute-start(bf16[128,7168]{1,0:T(8,128)(2,1)} %bitcast.10), channel_id=1, source_target_pairs={{0,4},{4,0},{8,12},{12,8},{16,20},{20,16},{24,28},{28,24},{1,5},{5... | collective-permute-start | bytes 5505032 | tf_op jit(solution)/shard_map/ppermute | solution.py:81
  0.5 10.2 %slice-start = ((s8[14680064]{0:T(1024)(128)(4,1)}), s8[4194304]{0:T(1024)(128)(4,1)S(1)}, s32[]{:S(2)}) async-start(s8[14680064]{0:T(1024)(128)(4,1)} %bitcast.8), calls=%async_computation | async-start | bytes 8388608
  0.5 10.2 %slice-start.1 = ((s8[14680064]{0:T(1024)(128)(4,1)}), s8[4194304]{0:T(1024)(128)(4,1)S(1)}, s32[]{:S(2)}) async-start(s8[14680064]{0:T(1024)(128)(4,1)} %bitcast.8), calls=%async_computation.1 | async-start | bytes 8388608
  0.5 10.2 %slice-start.2 = ((s8[14680064]{0:T(1024)(128)(4,1)}), s8[4194304]{0:T(1024)(128)(4,1)S(1)}, s32[]{:S(2)}) async-start(s8[14680064]{0:T(1024)(128)(4,1)} %bitcast.8), calls=%async_computation.2 | async-start | bytes 8388608
  0.5 10.2 %slice-start.3 = ((s8[14680064]{0:T(1024)(128)(4,1)}), s8[2097152]{0:T(1024)(128)(4,1)S(1)}, s32[]{:S(2)}) async-start(s8[14680064]{0:T(1024)(128)(4,1)} %bitcast.8), calls=%async_computation.3 | async-start | bytes 4194304
  1.9 5.1 %collective-permute-start = (bf16[4,7168]{1,0:T(4,128)(2,1)S(1)}, bf16[4,7168]{1,0:T(4,128)(2,1)S(1)}, u32[]{:S(2)}, u32[]{:S(2)}) collective-permute-start(bf16[4,7168]{1,0:T(4,128)(2,1)S(1)} %get-tuple-element.19.refs_0_), channel_id=1, source_target_pairs={{0,1},{1,0},{2,3},{3,2},{4,5},{5,4},{6,7},{7,6},{8,9},{9,8},{10,11... | collective-permute-start | bytes 172040 | tf_op jit(solution)/shard_map/ppermute | solution.py:81
  4.4 5.1 %collective-permute-start.2 = (bf16[4,7168]{1,0:T(4,128)(2,1)S(1)}, bf16[4,7168]{1,0:T(4,128)(2,1)S(1)}, u32[]{:S(2)}, u32[]{:S(2)}) collective-permute-start(bf16[4,7168]{1,0:T(4,128)(2,1)S(1)} %get-tuple-element.20), channel_id=1, source_target_pairs={{0,3},{1,2},{2,1},{3,0},{4,7},{5,6},{6,5},{7,4},{8,11},{9,10},{10,... | collective-permute-start | bytes 172040 | tf_op jit(solution)/shard_map/ppermute | solution.py:81
  5.9 4.7 %collective-permute-start.1 = (bf16[4,7168]{1,0:T(4,128)(2,1)S(1)}, bf16[4,7168]{1,0:T(4,128)(2,1)S(1)}, u32[]{:S(2)}, u32[]{:S(2)}) collective-permute-start(bf16[4,7168]{1,0:T(4,128)(2,1)S(1)} %get-tuple-element.20), channel_id=1, source_target_pairs={{0,2},{1,3},{2,0},{3,1},{4,6},{5,7},{6,4},{7,5},{8,10},{9,11},{10,... | collective-permute-start | bytes 172040 | tf_op jit(solution)/shard_map/ppermute | solution.py:81
  10.7 12.2 %copy-start = (bf16[1,128,7168]{2,1,0:T(8,128)(2,1)S(1)}, bf16[1,128,7168]{2,1,0:T(8,128)(2,1)}, u32[]{:S(2)}) copy-start(bf16[1,128,7168]{2,1,0:T(8,128)(2,1)} %param.12) | copy-start | bytes 5505028
  14.6 5.5 %collective-permute-start.5 = (bf16[16,512]{1,0:T(8,128)(2,1)S(1)}, bf16[16,512]{1,0:T(8,128)(2,1)S(1)}, u32[]{:S(2)}, u32[]{:S(2)}) collective-permute-start(bf16[16,512]{1,0:T(8,128)(2,1)S(1)} %activate.1.refs_0_), channel_id=1, source_target_pairs={{0,24},{4,28},{8,16},{12,20},{16,8},{20,12},{24,0},{28,4},{1,25},{... | collective-permute-start | bytes 49160 | tf_op jit(solution)/shard_map/ppermute | solution.py:81
  18.2 4.6 %collective-permute-start.4 = (bf16[16,512]{1,0:T(8,128)(2,1)S(1)}, bf16[16,512]{1,0:T(8,128)(2,1)S(1)}, u32[]{:S(2)}, u32[]{:S(2)}) collective-permute-start(bf16[16,512]{1,0:T(8,128)(2,1)S(1)} %activate.1.refs_0_), channel_id=1, source_target_pairs={{0,16},{4,20},{8,24},{12,28},{16,0},{20,4},{24,8},{28,12},{1,17},{... | collective-permute-start | bytes 49160 | tf_op jit(solution)/shard_map/ppermute | solution.py:81
  18.2 4.6 %collective-permute-start.3 = (bf16[16,512]{1,0:T(8,128)(2,1)S(1)}, bf16[16,512]{1,0:T(8,128)(2,1)S(1)}, u32[]{:S(2)}, u32[]{:S(2)}) collective-permute-start(bf16[16,512]{1,0:T(8,128)(2,1)S(1)} %activate.1.refs_0_), channel_id=1, source_target_pairs={{0,8},{4,12},{8,0},{12,4},{16,24},{20,28},{24,16},{28,20},{1,9},{5... | collective-permute-start | bytes 49160 | tf_op jit(solution)/shard_map/ppermute | solution.py:81
  22.9 19.6 %copy-start.1 = (f32[1,4]{1,0:T(1,128)S(1)}, f32[1,4]{1,0:T(1,128)}, u32[]{:S(2)}) copy-start(f32[1,4]{1,0:T(1,128)} %param.10) | copy-start | bytes 52
  24.0 7.1 %collective-permute-start.7 = (bf16[24,3584]{1,0:T(8,128)(2,1)S(1)}, bf16[24,3584]{1,0:T(8,128)(2,1)S(1)}, u32[]{:S(2)}, u32[]{:S(2)}) collective-permute-start(bf16[24,3584]{1,0:T(8,128)(2,1)S(1)} %get-tuple-element.24), channel_id=1, source_target_pairs={{0,1},{1,0},{2,3},{3,2},{4,5},{5,4},{6,7},{7,6},{8,9},{9,8},{10,11... | collective-permute-start | bytes 516104 | tf_op jit(solution)/shard_map/ppermute | solution.py:81
  25.4 8.2 %collective-permute-start.8 = (bf16[24,3584]{1,0:T(8,128)(2,1)S(1)}, bf16[24,3584]{1,0:T(8,128)(2,1)S(1)}, u32[]{:S(2)}, u32[]{:S(2)}) collective-permute-start(bf16[24,3584]{1,0:T(8,128)(2,1)S(1)} %get-tuple-element.25), channel_id=1, source_target_pairs={{0,2},{1,3},{2,0},{3,1},{4,6},{5,7},{6,4},{7,5},{8,10},{9,11},{10,... | collective-permute-start | bytes 516104 | tf_op jit(solution)/shard_map/ppermute | solution.py:81
  26.0 7.6 %collective-permute-start.9 = (bf16[24,3584]{1,0:T(8,128)(2,1)S(1)}, bf16[24,3584]{1,0:T(8,128)(2,1)S(1)}, u32[]{:S(2)}, u32[]{:S(2)}) collective-permute-start(bf16[24,3584]{1,0:T(8,128)(2,1)S(1)} %get-tuple-element.26), channel_id=1, source_target_pairs={{0,3},{1,2},{2,1},{3,0},{4,7},{5,6},{6,5},{7,4},{8,11},{9,10},{10,... | collective-permute-start | bytes 516104 | tf_op jit(solution)/shard_map/ppermute | solution.py:81
  34.0 5.5 %collective-permute-start.10 = (bf16[4,7168]{1,0:T(4,128)(2,1)S(1)}, bf16[4,7168]{1,0:T(4,128)(2,1)S(1)}, u32[]{:S(2)}, u32[]{:S(2)}) collective-permute-start(bf16[4,7168]{1,0:T(4,128)(2,1)S(1)} %get-tuple-element.28), channel_id=1, source_target_pairs={{0,8},{4,12},{8,0},{12,4},{16,24},{20,28},{24,16},{28,20},{1,9},{5... | collective-permute-start | bytes 172040 | tf_op jit(solution)/shard_map/ppermute | solution.py:81
  34.1 5.4 %collective-permute-start.11 = (bf16[4,7168]{1,0:T(4,128)(2,1)S(1)}, bf16[4,7168]{1,0:T(4,128)(2,1)S(1)}, u32[]{:S(2)}, u32[]{:S(2)}) collective-permute-start(bf16[4,7168]{1,0:T(4,128)(2,1)S(1)} %get-tuple-element.29), channel_id=1, source_target_pairs={{0,16},{4,20},{8,24},{12,28},{16,0},{20,4},{24,8},{28,12},{1,17},{... | collective-permute-start | bytes 172040 | tf_op jit(solution)/shard_map/ppermute | solution.py:81
  36.5 6.0 %collective-permute-start.12 = (bf16[4,7168]{1,0:T(4,128)(2,1)S(1)}, bf16[4,7168]{1,0:T(4,128)(2,1)S(1)}, u32[]{:S(2)}, u32[]{:S(2)}) collective-permute-start(bf16[4,7168]{1,0:T(4,128)(2,1)S(1)} %get-tuple-element.30), channel_id=1, source_target_pairs={{0,24},{4,28},{8,16},{12,20},{16,8},{20,12},{24,0},{28,4},{1,25},{... | collective-permute-start | bytes 172040 | tf_op jit(solution)/shard_map/ppermute | solution.py:81

commit v3 on v2

--- a/solution.py
+++ b/solution.py
@@ -139,9 +139,11 @@
         )
 
 
-def flag_body(chips, row_count, owner, after, flags, placing, owner_ref, sems):
+def flag_body(chips, row_count, owner, weight, after, flags, placing, column_ref, owner_ref, weight_ref, sems):
     owner_copy = pltpu.make_async_copy(owner, owner_ref, sems.at[0])
     owner_copy.start()
+    weight_copy = pltpu.make_async_copy(weight, weight_ref, sems.at[1])
+    weight_copy.start()
     shape = placing.shape[1:]
     row, column = (lax.broadcasted_iota(jnp.int32, shape, axis) for axis in (0, 1))
     block, used = 2 * CAP * chips, shape[0] // 2
@@ -159,6 +161,31 @@
             hit = jnp.where(owner_ref[0, bucket] == (group ^ which), 1.0, 0.0)
             values = jnp.where(row == which * BUCKETS + bucket, hit, values)
     flags[...] = values
+    weight_copy.wait()
+    square = (row_count, row_count)
+    same = lax.broadcasted_iota(jnp.int32, square, 0) == lax.broadcasted_iota(jnp.int32, square, 1)
+    picked = jnp.sum(jnp.where(same, weight_ref[...], 0.0), axis=1, keepdims=True)
+    column_ref[...] = jnp.broadcast_to(picked, column_ref.shape)
+
+
+def finish_body(column_ref, *refs):
+    shares, out, staged, sems = refs[:-3], refs[-3], refs[-2], refs[-1]
+    width = staged.shape[1]
+    weight = column_ref[:, 0:1]
+    half = width // 2
+    copies = []
+    for part in range(2):
+        here = pl.ds(part * half, half)
+        total = 0.0
+        for share in shares:
+            total = total + share[:, part * half : (part + 1) * half].astype(jnp.float32)
+        staged[:, part * half : (part + 1) * half] = (total * weight).astype(jnp.bfloat16)
+        copies.append(
+            pltpu.make_async_copy(staged.at[:, here], out.at[:, here], sems.at[part])
+        )
+        copies[-1].start()
+    for copy in copies:
+        copy.wait()
 
 
 def activate_body(devices, weights, code_ref, *refs):
@@ -204,7 +231,7 @@
                 placing[chip], chosen.astype(jnp.bfloat16), preferred_element_type=jnp.float32
             )
     placed = [part.astype(jnp.bfloat16) for part in placed]
-    step = half // 7 if half % (7 * 128) == 0 else half
+    step = half // 2 if half % 512 == 0 else half
     for start in range(0, half, step):
         out = 0.0
         for rows_at, column in ((0, start), (used, half + start)):
@@ -296,18 +323,23 @@
     )(*in_hbm(route.reshape(1, row_count), rows, norm_gain.reshape(1, width)))
     arrived = exchange([packed[bits // shards] for bits in range(devices)], "exp", 1)
     other_piece = swap(own_piece, "grp", 1)
-    flags, spots = pl.pallas_call(
+    flags, spots, weight_column = pl.pallas_call(
         functools.partial(flag_body, chips, row_count),
         out_shape=[
             pltpu.VMEM((8, CODE), jnp.float32),
             pltpu.VMEM((chips, 2 * devices * block, devices * row_count), jnp.bfloat16),
+            pltpu.VMEM((row_count, CODE), jnp.float32),
         ],
-        in_specs=[HBM, ANY],
-        out_specs=[VMEM] * 2,
-        scratch_shapes=[pltpu.SMEM((1, owner.shape[0]), jnp.int32), pltpu.SemaphoreType.DMA((1,))],
+        in_specs=[HBM, HBM, ANY],
+        out_specs=[VMEM] * 3,
+        scratch_shapes=[
+            pltpu.SMEM((1, owner.shape[0]), jnp.int32),
+            pltpu.VMEM((1, row_count), jnp.float32),
+            pltpu.SemaphoreType.DMA((2,)),
+        ],
         compiler_params=limit(2),
         name="flag",
-    )(*in_hbm(owner.reshape(1, -1)), *held(code))
+    )(*in_hbm(owner.reshape(1, -1), route_weight), *held(code))
     act = pl.pallas_call(
         functools.partial(activate_body, devices),
         out_shape=pltpu.VMEM((devices * row_count, units), jnp.bfloat16),
@@ -345,10 +377,18 @@
         compiler_params=limit(8),
         name="combine",
     )(*held(placing, *returned))
-    combined = 0.0
-    for share in exchange(sums, "grp", PAIR):
-        combined = combined + share.astype(jnp.float32)
-    result = (combined * route_weight[0][:, None]).astype(jnp.bfloat16)
+    result = pl.pallas_call(
+        finish_body,
+        out_shape=jax.ShapeDtypeStruct((row_count, width), jnp.bfloat16),
+        in_specs=[VMEM] * (1 + chips),
+        out_specs=HBM,
+        scratch_shapes=[
+            pltpu.VMEM((row_count, width), jnp.bfloat16),
+            pltpu.SemaphoreType.DMA((2,)),
+        ],
+        compiler_params=limit(2),
+        name="finish",
+    )(*held(weight_column, *exchange(sums, "grp", PAIR)))
     return result.reshape(1, row_count, width)
 
 

time: 43.3 us -> 43.4 us (level)
  Pallas kernels: 7.51 us -> 8.43 us
  other arithmetic: 0.71 us -> 0.01 us
    pallas_call x0 -> x1, Pallas kernels: none -> 0.71 us  [move_rows(): pl.pallas_call(finish_body, out_shape=jax.ShapeDtypeStruct((row_count, wi...]
    reshape x1 -> x0, other arithmetic: 0.71 us -> none  [move_rows(): return result.reshape(1, row_count, width)]
where the time goes in v3:
time: 43.4 us; the launch traced here: 43.3 us
  waiting for transfers between devices  17.8 us (41%)
  starting transfers between devices  17 us (39%)
  Pallas kernels  8.43 us (19%)
    ppermute x13, waiting for transfers between devices, swap(): return lax.ppermute(value, axis, [(i, i ^ bits) for i in range(size)])  17.8 us
    ppermute x13, starting transfers between devices, swap(): return lax.ppermute(value, axis, [(i, i ^ bits) for i in range(size)])  17 us
    pallas_call x1, Pallas kernels, move_rows(): pl.pallas_call(functools.partial(activate_body, devices), out_shape=pltpu...  3.91 us
    pallas_call x1, Pallas kernels, move_rows(): pl.pallas_call(functools.partial(prepare_body, shards), out_shape=[row_bl...  1.35 us
    pallas_call x1, Pallas kernels, move_rows(): pl.pallas_call(functools.partial(down_body, devices, chips), out_shape=[h...  1.2 us
  transfers between devices with their start and end apart: 13, of which 9 were waited for; matrix products, arithmetic and copies ran while one was open for 0% of the time, Pallas kernels for 14%

profile of v3, /device:TPU:0, one launch (start us, length us, event | category | flops | bytes accessed | tf_op | source)
XLA Modules:
  0.0 43.3 jit_solution(10779377180343506302)
XLA Ops:
  0.0 0.5 %collective-permute-start.6 = (bf16[128,7168]{1,0:T(8,128)(2,1)}, bf16[128,7168]{1,0:T(8,128)(2,1)S(1)}, u32[]{:S(2)}, u32[]{:S(2)}) collective-permute-start(bf16[128,7168]{1,0:T(8,128)(2,1)} %bitcast.8), channel_id=1, source_target_pairs={{0,4},{4,0},{8,12},{12,8},{16,20},{20,16},{24,28},{28,24},{1,5},{5... | collective-permute-start | bytes 5505032 | tf_op jit(solution)/shard_map/ppermute | solution.py:81
  0.5 0.0 slice-start
  0.5 0.0 slice-start.1
  0.5 0.0 slice-start.2
  0.5 0.0 slice-start.3
  0.5 1.4 %prepare.1 = (bf16[4,7168]{1,0:T(4,128)(2,1)S(1)}, bf16[4,7168]{1,0:T(4,128)(2,1)S(1)}, f32[8,128]{1,0:T(8,128)S(1)}) custom-call(s32[1,4]{1,0:T(1,128)} %bitcast.13, bf16[4,7168]{1,0:T(4,128)(2,1)} %bitcast.11, f32[1,7168]{1,0:T(1,128)} %bitcast.12), custom_call_target="tpu_custom_call" | custom-call | flops 10000000000 | bytes 20000000 | tf_op jit(solution)/shard_map/prepare/pallas_call | solution.py:309
  1.9 2.6 %collective-permute-start = (bf16[4,7168]{1,0:T(4,128)(2,1)S(1)}, bf16[4,7168]{1,0:T(4,128)(2,1)S(1)}, u32[]{:S(2)}, u32[]{:S(2)}) collective-permute-start(bf16[4,7168]{1,0:T(4,128)(2,1)S(1)} %get-tuple-element.21.refs_0_), channel_id=1, source_target_pairs={{0,1},{1,0},{2,3},{3,2},{4,5},{5,4},{6,7},{7,6},{8,9},{9,8},{10,11... | collective-permute-start | bytes 172040 | tf_op jit(solution)/shard_map/ppermute | solution.py:81
  4.4 1.5 %collective-permute-start.2 = (bf16[4,7168]{1,0:T(4,128)(2,1)S(1)}, bf16[4,7168]{1,0:T(4,128)(2,1)S(1)}, u32[]{:S(2)}, u32[]{:S(2)}) collective-permute-start(bf16[4,7168]{1,0:T(4,128)(2,1)S(1)} %get-tuple-element.22), channel_id=1, source_target_pairs={{0,3},{1,2},{2,1},{3,0},{4,7},{5,6},{6,5},{7,4},{8,11},{9,10},{10,... | collective-permute-start | bytes 172040 | tf_op jit(solution)/shard_map/ppermute | solution.py:81
  5.9 0.1 collective-permute-start.1
  6.0 1.0 %collective-permute-done.refs_1_ = bf16[4,7168]{1,0:T(4,128)(2,1)S(1)} collective-permute-done((bf16[4,7168]{1,0:T(4,128)(2,1)S(1)}, bf16[4,7168]{1,0:T(4,128)(2,1)S(1)}, u32[]{:S(2)}, u32[]{:S(2)}) %collective-permute-start) | collective-permute-done | bytes 57376 | tf_op jit(solution)/shard_map/ppermute | solution.py:81
  7.0 2.5 %collective-permute-done.2.refs_3_ = bf16[4,7168]{1,0:T(4,128)(2,1)S(1)} collective-permute-done((bf16[4,7168]{1,0:T(4,128)(2,1)S(1)}, bf16[4,7168]{1,0:T(4,128)(2,1)S(1)}, u32[]{:S(2)}, u32[]{:S(2)}) %collective-permute-start.2) | collective-permute-done | bytes 57376 | tf_op jit(solution)/shard_map/ppermute | solution.py:81
  9.5 1.1 %collective-permute-done.1.refs_2_ = bf16[4,7168]{1,0:T(4,128)(2,1)S(1)} collective-permute-done((bf16[4,7168]{1,0:T(4,128)(2,1)S(1)}, bf16[4,7168]{1,0:T(4,128)(2,1)S(1)}, u32[]{:S(2)}, u32[]{:S(2)}) %collective-permute-start.1) | collective-permute-done | bytes 57376 | tf_op jit(solution)/shard_map/ppermute | solution.py:81
  10.7 0.0 slice-done
  10.7 0.0 slice-done.1
  10.7 0.0 slice-done.2
  10.7 0.0 slice-done.3
  10.7 0.0 copy-start
  10.7 3.9 %activate.1.refs_0_ = bf16[16,512]{1,0:T(8,128)(2,1)S(1)} custom-call(bf16[2,512,7168]{2,1,0:T(8,128)(2,1)S(1)} %bitcast.7, f32[8,128]{1,0:T(8,128)S(1)} %get-tuple-element.19.after.code_ref, bf16[4,7168]{1,0:T(4,128)(2,1)S(1)} %get-tuple-element.21.refs_0_, bf16[4,7168]{1,0:T(4,128)(2,1)S(1)} %collective-permute-done.refs_1_, ...), custom_call_target="tpu_custom_call" | custom-call | tf_op jit(solution)/shard_map/activate/pallas_call | solution.py:343
  14.6 3.6 %collective-permute-start.5 = (bf16[16,512]{1,0:T(8,128)(2,1)S(1)}, bf16[16,512]{1,0:T(8,128)(2,1)S(1)}, u32[]{:S(2)}, u32[]{:S(2)}) collective-permute-start(bf16[16,512]{1,0:T(8,128)(2,1)S(1)} %activate.1.refs_0_), channel_id=1, source_target_pairs={{0,24},{4,28},{8,16},{12,20},{16,8},{20,12},{24,0},{28,4},{1,25},{... | collective-permute-start | bytes 49160 | tf_op jit(solution)/shard_map/ppermute | solution.py:81
  18.2 0.0 collective-permute-start.4
  18.2 0.8 %collective-permute-start.3 = (bf16[16,512]{1,0:T(8,128)(2,1)S(1)}, bf16[16,512]{1,0:T(8,128)(2,1)S(1)}, u32[]{:S(2)}, u32[]{:S(2)}) collective-permute-start(bf16[16,512]{1,0:T(8,128)(2,1)S(1)} %activate.1.refs_0_), channel_id=1, source_target_pairs={{0,8},{4,12},{8,0},{12,4},{16,24},{20,28},{24,16},{28,20},{1,9},{5... | collective-permute-start | bytes 49160 | tf_op jit(solution)/shard_map/ppermute | solution.py:81
  19.0 0.8 %flag.1 = (f32[8,128]{1,0:T(8,128)S(1)}, bf16[4,192,16]{2,1,0:T(8,128)(2,1)S(1)}, f32[4,128]{1,0:T(4,128)S(1)}) custom-call(s32[1,8]{1,0:T(1,128)} %bitcast.10, f32[1,4]{1,0:T(1,128)} %weight.1, f32[8,128]{1,0:T(8,128)S(1)} %get-tuple-element.19.after.code_ref), custom_call_target="tpu_custom_call" | custom-call | tf_op jit(solution)/shard_map/flag/pallas_call | solution.py:326
  19.8 0.4 collective-permute-done.5.refs_3_
  20.2 2.7 %collective-permute-done.4.refs_2_ = bf16[16,512]{1,0:T(8,128)(2,1)S(1)} collective-permute-done((bf16[16,512]{1,0:T(8,128)(2,1)S(1)}, bf16[16,512]{1,0:T(8,128)(2,1)S(1)}, u32[]{:S(2)}, u32[]{:S(2)}) %collective-permute-start.4) | collective-permute-done | bytes 16416 | tf_op jit(solution)/shard_map/ppermute | solution.py:81
  22.9 0.0 collective-permute-done.3.refs_1_
  22.9 0.0 collective-permute-done.6.other
  22.9 0.0 copy-done
  22.9 1.2 %down.1 = (bf16[24,3584]{1,0:T(8,128)(2,1)S(1)}, bf16[24,3584]{1,0:T(8,128)(2,1)S(1)}, bf16[24,3584]{1,0:T(8,128)(2,1)S(1)}, bf16[24,3584]{1,0:T(8,128)(2,1)S(1)}) custom-call(bf16[128,7168]{1,0:T(8,128)(2,1)S(1)} %bitcast.9, bf16[128,7168]{1,0:T(8,128)(2,1)S(1)} %collective-permute-done.6.other, f32[8,128]{1,0:T(8,128)S(1)} %get-tuple-element.23.flags, ...), custom_call_target="tpu_custom_call" | custom-call | tf_op jit(solution)/shard_map/down/pallas_call | solution.py:354
  24.1 1.4 %collective-permute-start.7 = (bf16[24,3584]{1,0:T(8,128)(2,1)S(1)}, bf16[24,3584]{1,0:T(8,128)(2,1)S(1)}, u32[]{:S(2)}, u32[]{:S(2)}) collective-permute-start(bf16[24,3584]{1,0:T(8,128)(2,1)S(1)} %get-tuple-element.26), channel_id=1, source_target_pairs={{0,1},{1,0},{2,3},{3,2},{4,5},{5,4},{6,7},{7,6},{8,9},{9,8},{10,11... | collective-permute-start | bytes 516104 | tf_op jit(solution)/shard_map/ppermute | solution.py:81
  25.5 0.6 %collective-permute-start.8 = (bf16[24,3584]{1,0:T(8,128)(2,1)S(1)}, bf16[24,3584]{1,0:T(8,128)(2,1)S(1)}, u32[]{:S(2)}, u32[]{:S(2)}) collective-permute-start(bf16[24,3584]{1,0:T(8,128)(2,1)S(1)} %get-tuple-element.27), channel_id=1, source_target_pairs={{0,2},{1,3},{2,0},{3,1},{4,6},{5,7},{6,4},{7,5},{8,10},{9,11},{10,... | collective-permute-start | bytes 516104 | tf_op jit(solution)/shard_map/ppermute | solution.py:81
  26.1 1.5 %collective-permute-start.9 = (bf16[24,3584]{1,0:T(8,128)(2,1)S(1)}, bf16[24,3584]{1,0:T(8,128)(2,1)S(1)}, u32[]{:S(2)}, u32[]{:S(2)}) collective-permute-start(bf16[24,3584]{1,0:T(8,128)(2,1)S(1)} %get-tuple-element.28), channel_id=1, source_target_pairs={{0,3},{1,2},{2,1},{3,0},{4,7},{5,6},{6,5},{7,4},{8,11},{9,10},{10,... | collective-permute-start | bytes 516104 | tf_op jit(solution)/shard_map/ppermute | solution.py:81
  27.6 0.1 place.1.placing
  27.7 3.4 %collective-permute-done.7.refs_1_ = bf16[24,3584]{1,0:T(8,128)(2,1)S(1)} collective-permute-done((bf16[24,3584]{1,0:T(8,128)(2,1)S(1)}, bf16[24,3584]{1,0:T(8,128)(2,1)S(1)}, u32[]{:S(2)}, u32[]{:S(2)}) %collective-permute-start.7) | collective-permute-done | bytes 172064 | tf_op jit(solution)/shard_map/ppermute | solution.py:81
  31.2 2.5 %collective-permute-done.8.refs_2_ = bf16[24,3584]{1,0:T(8,128)(2,1)S(1)} collective-permute-done((bf16[24,3584]{1,0:T(8,128)(2,1)S(1)}, bf16[24,3584]{1,0:T(8,128)(2,1)S(1)}, u32[]{:S(2)}, u32[]{:S(2)}) %collective-permute-start.8) | collective-permute-done | bytes 172064 | tf_op jit(solution)/shard_map/ppermute | solution.py:81
  33.7 0.0 collective-permute-done.9.refs_3_
  33.7 0.4 combine.1
  34.1 0.1 collective-permute-start.10
  34.2 2.4 %collective-permute-start.11 = (bf16[4,7168]{1,0:T(4,128)(2,1)S(1)}, bf16[4,7168]{1,0:T(4,128)(2,1)S(1)}, u32[]{:S(2)}, u32[]{:S(2)}) collective-permute-start(bf16[4,7168]{1,0:T(4,128)(2,1)S(1)} %get-tuple-element.31), channel_id=1, source_target_pairs={{0,16},{4,20},{8,24},{12,28},{16,0},{20,4},{24,8},{28,12},{1,17},{... | collective-permute-start | bytes 172040 | tf_op jit(solution)/shard_map/ppermute | solution.py:81
  36.6 1.9 %collective-permute-start.12 = (bf16[4,7168]{1,0:T(4,128)(2,1)S(1)}, bf16[4,7168]{1,0:T(4,128)(2,1)S(1)}, u32[]{:S(2)}, u32[]{:S(2)}) collective-permute-start(bf16[4,7168]{1,0:T(4,128)(2,1)S(1)} %get-tuple-element.32), channel_id=1, source_target_pairs={{0,24},{4,28},{8,16},{12,20},{16,8},{20,12},{24,0},{28,4},{1,25},{... | collective-permute-start | bytes 172040 | tf_op jit(solution)/shard_map/ppermute | solution.py:81
  38.6 1.0 %collective-permute-done.10.refs_1_ = bf16[4,7168]{1,0:T(4,128)(2,1)S(1)} collective-permute-done((bf16[4,7168]{1,0:T(4,128)(2,1)S(1)}, bf16[4,7168]{1,0:T(4,128)(2,1)S(1)}, u32[]{:S(2)}, u32[]{:S(2)}) %collective-permute-start.10) | collective-permute-done | bytes 57376 | tf_op jit(solution)/shard_map/ppermute | solution.py:81
  39.6 0.0 collective-permute-done.11.refs_2_
  39.6 3.0 %collective-permute-done.12.refs_3_ = bf16[4,7168]{1,0:T(4,128)(2,1)S(1)} collective-permute-done((bf16[4,7168]{1,0:T(4,128)(2,1)S(1)}, bf16[4,7168]{1,0:T(4,128)(2,1)S(1)}, u32[]{:S(2)}, u32[]{:S(2)}) %collective-permute-start.12) | collective-permute-done | bytes 57376 | tf_op jit(solution)/shard_map/ppermute | solution.py:81
  42.6 0.7 %finish.1 = bf16[4,7168]{1,0:T(4,128)(2,1)} custom-call(f32[4,128]{1,0:T(4,128)S(1)} %get-tuple-element.20.column_ref, bf16[4,7168]{1,0:T(4,128)(2,1)S(1)} %get-tuple-element.29.refs_0_, bf16[4,7168]{1,0:T(4,128)(2,1)S(1)} %collective-permute-done.10.refs_1_, bf16[4,7168]{1,0:T(4,128)(2,1)S(1)} %collective-permute-done.11.refs_2_, ...), custom_call_target="tpu_custom_call" | custom-call | tf_op jit(solution)/shard_map/finish/pallas_call | solution.py:380
  (1 shorter events, 0.0 us)
Async XLA Ops:
  0.0 22.9 %collective-permute-start.6 = (bf16[128,7168]{1,0:T(8,128)(2,1)}, bf16[128,7168]{1,0:T(8,128)(2,1)S(1)}, u32[]{:S(2)}, u32[]{:S(2)}) collective-permute-start(bf16[128,7168]{1,0:T(8,128)(2,1)} %bitcast.8), channel_id=1, source_target_pairs={{0,4},{4,0},{8,12},{12,8},{16,20},{20,16},{24,28},{28,24},{1,5},{5... | collective-permute-start | bytes 5505032 | tf_op jit(solution)/shard_map/ppermute | solution.py:81
  0.5 10.2 %slice-start = ((s8[14680064]{0:T(1024)(128)(4,1)}), s8[4194304]{0:T(1024)(128)(4,1)S(1)}, s32[]{:S(2)}) async-start(s8[14680064]{0:T(1024)(128)(4,1)} %bitcast.6), calls=%async_computation | async-start | bytes 8388608
  0.5 10.2 %slice-start.1 = ((s8[14680064]{0:T(1024)(128)(4,1)}), s8[4194304]{0:T(1024)(128)(4,1)S(1)}, s32[]{:S(2)}) async-start(s8[14680064]{0:T(1024)(128)(4,1)} %bitcast.6), calls=%async_computation.1 | async-start | bytes 8388608
  0.5 10.2 %slice-start.2 = ((s8[14680064]{0:T(1024)(128)(4,1)}), s8[4194304]{0:T(1024)(128)(4,1)S(1)}, s32[]{:S(2)}) async-start(s8[14680064]{0:T(1024)(128)(4,1)} %bitcast.6), calls=%async_computation.2 | async-start | bytes 8388608
  0.5 10.2 %slice-start.3 = ((s8[14680064]{0:T(1024)(128)(4,1)}), s8[2097152]{0:T(1024)(128)(4,1)S(1)}, s32[]{:S(2)}) async-start(s8[14680064]{0:T(1024)(128)(4,1)} %bitcast.6), calls=%async_computation.3 | async-start | bytes 4194304
  1.9 5.1 %collective-permute-start = (bf16[4,7168]{1,0:T(4,128)(2,1)S(1)}, bf16[4,7168]{1,0:T(4,128)(2,1)S(1)}, u32[]{:S(2)}, u32[]{:S(2)}) collective-permute-start(bf16[4,7168]{1,0:T(4,128)(2,1)S(1)} %get-tuple-element.21.refs_0_), channel_id=1, source_target_pairs={{0,1},{1,0},{2,3},{3,2},{4,5},{5,4},{6,7},{7,6},{8,9},{9,8},{10,11... | collective-permute-start | bytes 172040 | tf_op jit(solution)/shard_map/ppermute | solution.py:81
  4.4 5.1 %collective-permute-start.2 = (bf16[4,7168]{1,0:T(4,128)(2,1)S(1)}, bf16[4,7168]{1,0:T(4,128)(2,1)S(1)}, u32[]{:S(2)}, u32[]{:S(2)}) collective-permute-start(bf16[4,7168]{1,0:T(4,128)(2,1)S(1)} %get-tuple-element.22), channel_id=1, source_target_pairs={{0,3},{1,2},{2,1},{3,0},{4,7},{5,6},{6,5},{7,4},{8,11},{9,10},{10,... | collective-permute-start | bytes 172040 | tf_op jit(solution)/shard_map/ppermute | solution.py:81
  5.9 4.7 %collective-permute-start.1 = (bf16[4,7168]{1,0:T(4,128)(2,1)S(1)}, bf16[4,7168]{1,0:T(4,128)(2,1)S(1)}, u32[]{:S(2)}, u32[]{:S(2)}) collective-permute-start(bf16[4,7168]{1,0:T(4,128)(2,1)S(1)} %get-tuple-element.22), channel_id=1, source_target_pairs={{0,2},{1,3},{2,0},{3,1},{4,6},{5,7},{6,4},{7,5},{8,10},{9,11},{10,... | collective-permute-start | bytes 172040 | tf_op jit(solution)/shard_map/ppermute | solution.py:81
  10.7 12.2 %copy-start = (bf16[1,128,7168]{2,1,0:T(8,128)(2,1)S(1)}, bf16[1,128,7168]{2,1,0:T(8,128)(2,1)}, u32[]{:S(2)}) copy-start(bf16[1,128,7168]{2,1,0:T(8,128)(2,1)} %param.12) | copy-start | bytes 5505028
  14.6 5.5 %collective-permute-start.5 = (bf16[16,512]{1,0:T(8,128)(2,1)S(1)}, bf16[16,512]{1,0:T(8,128)(2,1)S(1)}, u32[]{:S(2)}, u32[]{:S(2)}) collective-permute-start(bf16[16,512]{1,0:T(8,128)(2,1)S(1)} %activate.1.refs_0_), channel_id=1, source_target_pairs={{0,24},{4,28},{8,16},{12,20},{16,8},{20,12},{24,0},{28,4},{1,25},{... | collective-permute-start | bytes 49160 | tf_op jit(solution)/shard_map/ppermute | solution.py:81
  18.2 4.6 %collective-permute-start.4 = (bf16[16,512]{1,0:T(8,128)(2,1)S(1)}, bf16[16,512]{1,0:T(8,128)(2,1)S(1)}, u32[]{:S(2)}, u32[]{:S(2)}) collective-permute-start(bf16[16,512]{1,0:T(8,128)(2,1)S(1)} %activate.1.refs_0_), channel_id=1, source_target_pairs={{0,16},{4,20},{8,24},{12,28},{16,0},{20,4},{24,8},{28,12},{1,17},{... | collective-permute-start | bytes 49160 | tf_op jit(solution)/shard_map/ppermute | solution.py:81
  18.2 4.6 %collective-permute-start.3 = (bf16[16,512]{1,0:T(8,128)(2,1)S(1)}, bf16[16,512]{1,0:T(8,128)(2,1)S(1)}, u32[]{:S(2)}, u32[]{:S(2)}) collective-permute-start(bf16[16,512]{1,0:T(8,128)(2,1)S(1)} %activate.1.refs_0_), channel_id=1, source_target_pairs={{0,8},{4,12},{8,0},{12,4},{16,24},{20,28},{24,16},{28,20},{1,9},{5... | collective-permute-start | bytes 49160 | tf_op jit(solution)/shard_map/ppermute | solution.py:81
  24.1 7.1 %collective-permute-start.7 = (bf16[24,3584]{1,0:T(8,128)(2,1)S(1)}, bf16[24,3584]{1,0:T(8,128)(2,1)S(1)}, u32[]{:S(2)}, u32[]{:S(2)}) collective-permute-start(bf16[24,3584]{1,0:T(8,128)(2,1)S(1)} %get-tuple-element.26), channel_id=1, source_target_pairs={{0,1},{1,0},{2,3},{3,2},{4,5},{5,4},{6,7},{7,6},{8,9},{9,8},{10,11... | collective-permute-start | bytes 516104 | tf_op jit(solution)/shard_map/ppermute | solution.py:81
  25.5 8.2 %collective-permute-start.8 = (bf16[24,3584]{1,0:T(8,128)(2,1)S(1)}, bf16[24,3584]{1,0:T(8,128)(2,1)S(1)}, u32[]{:S(2)}, u32[]{:S(2)}) collective-permute-start(bf16[24,3584]{1,0:T(8,128)(2,1)S(1)} %get-tuple-element.27), channel_id=1, source_target_pairs={{0,2},{1,3},{2,0},{3,1},{4,6},{5,7},{6,4},{7,5},{8,10},{9,11},{10,... | collective-permute-start | bytes 516104 | tf_op jit(solution)/shard_map/ppermute | solution.py:81
  26.1 7.6 %collective-permute-start.9 = (bf16[24,3584]{1,0:T(8,128)(2,1)S(1)}, bf16[24,3584]{1,0:T(8,128)(2,1)S(1)}, u32[]{:S(2)}, u32[]{:S(2)}) collective-permute-start(bf16[24,3584]{1,0:T(8,128)(2,1)S(1)} %get-tuple-element.28), channel_id=1, source_target_pairs={{0,3},{1,2},{2,1},{3,0},{4,7},{5,6},{6,5},{7,4},{8,11},{9,10},{10,... | collective-permute-start | bytes 516104 | tf_op jit(solution)/shard_map/ppermute | solution.py:81
  34.1 5.5 %collective-permute-start.10 = (bf16[4,7168]{1,0:T(4,128)(2,1)S(1)}, bf16[4,7168]{1,0:T(4,128)(2,1)S(1)}, u32[]{:S(2)}, u32[]{:S(2)}) collective-permute-start(bf16[4,7168]{1,0:T(4,128)(2,1)S(1)} %get-tuple-element.30), channel_id=1, source_target_pairs={{0,8},{4,12},{8,0},{12,4},{16,24},{20,28},{24,16},{28,20},{1,9},{5... | collective-permute-start | bytes 172040 | tf_op jit(solution)/shard_map/ppermute | solution.py:81
  34.2 5.4 %collective-permute-start.11 = (bf16[4,7168]{1,0:T(4,128)(2,1)S(1)}, bf16[4,7168]{1,0:T(4,128)(2,1)S(1)}, u32[]{:S(2)}, u32[]{:S(2)}) collective-permute-start(bf16[4,7168]{1,0:T(4,128)(2,1)S(1)} %get-tuple-element.31), channel_id=1, source_target_pairs={{0,16},{4,20},{8,24},{12,28},{16,0},{20,4},{24,8},{28,12},{1,17},{... | collective-permute-start | bytes 172040 | tf_op jit(solution)/shard_map/ppermute | solution.py:81
  36.6 6.0 %collective-permute-start.12 = (bf16[4,7168]{1,0:T(4,128)(2,1)S(1)}, bf16[4,7168]{1,0:T(4,128)(2,1)S(1)}, u32[]{:S(2)}, u32[]{:S(2)}) collective-permute-start(bf16[4,7168]{1,0:T(4,128)(2,1)S(1)} %get-tuple-element.32), channel_id=1, source_target_pairs={{0,24},{4,28},{8,16},{12,20},{16,8},{20,12},{24,0},{28,4},{1,25},{... | collective-permute-start | bytes 172040 | tf_op jit(solution)/shard_map/ppermute | solution.py:81
